TPU v7x, 32 devices: a whole 2x2x4 slice. The times are simulated.
32 devices in a mesh: seq: 8 (over z, y), batch: 4 (over x, core).
Axes of the slice: x: 2, y: 2, z: 4, core: 2. Of those that a mesh axis runs over, the one named last changes fastest.
Arguments:
- tokens: bfloat16 [16, 1024, 896], P('batch', 'seq'), may hold values from -6 to 6
- doc_start: int32 [16, 1024], P('batch', 'seq'), may hold values from 0 to 1023, as said below
- neighbours: bfloat16 [16, 16, 256, 896], P('batch', 'seq'), may hold values from -6 to 6
- qkv_weight: bfloat16 [896, 6144], P(None, ('seq', 'batch')), may hold values from -0.25 to 0.25
- out_weight: bfloat16 [1024, 1792], P(None, ('seq', 'batch')), may hold values from -0.5 to 0.5
- ff_in: bfloat16 [896, 3584], P(None, ('seq', 'batch')), may hold values from -0.1875 to 0.1875
- ff_out: bfloat16 [3584, 896], P(('seq', 'batch')), may hold values from -0.09375 to 0.09375
- gains: float32 [3, 896], replicated, may hold values from 0.25 to 1.75
- cotangent: bfloat16 [16, 1024, 896], P('batch', 'seq'), may hold values from -6 to 6
Outputs:
- output: bfloat16 [16, 1024, 896], P('batch', 'seq')
- grad_tokens: float32 [16, 1024, 896], P('batch', 'seq')
- grad_neighbours: float32 [16, 16, 256, 896], P('batch', 'seq')
- grad_qkv_weight: float32 [896, 6144], P(None, ('seq', 'batch'))
- grad_out_weight: float32 [1024, 1792], P(None, ('seq', 'batch'))
- grad_ff_in: float32 [896, 3584], P(None, ('seq', 'batch'))
- grad_ff_out: float32 [3584, 896], P(('seq', 'batch'))
- grad_gains: float32 [3, 896], replicated
Inputs may be any that keep to these rules, and one draw needn't show every extreme that they name: doc_start[b, p] is where the document holding token p of sequence b begins: doc_start[b, 0] = 0, and doc_start[b, p] is p or doc_start[b, p - 1]. The last position of every sequence begins a document of one token.
All inputs are finite; a program needn't handle non-finite values.
Results may differ from a plain program's by a relative error of at most 0.025.
The roundings to bfloat16 on the way count: a program that leaves them out, or rounds other values in their place, can miss the bound.
Values may be sent and summed in bfloat16 or wider, within the bound.
No kernel may reach another device: no remote copies, remote signals or barrier semaphores. Data moves between devices by JAX's collectives and lax.ppermute only.
A program may use at most 384 MiB of HBM per device.

v0:
```python
import math

import jax
import jax.numpy as jnp
from jax import lax
from jax.sharding import PartitionSpec as P

HEADS = 16
HEAD = 64
SPAN = 64


score_scale = 0.125
gelu_coef = math.sqrt(2.0 / math.pi)
norm_eps = 1e-05


def passed_along(value, axis, steps):
    count = lax.axis_size(axis)
    leading, last = (max(0, -steps), min(count, count - steps))
    return lax.ppermute(value, axis, [(source, source + steps) for source in range(leading, last)])


def heads_of(values):
    return values.reshape(values.shape[:-1] + (HEADS, HEAD))


def rope_tables(relative):
    half_size = HEAD // 2
    frequency = jnp.exp(jnp.arange(half_size, dtype=jnp.float32) * (-math.log(10000.0) / half_size))
    angles = relative[..., None] * frequency
    return (jnp.cos(angles), jnp.sin(angles))


def rotate(values, cosine_table, sine_table, turn_sign):
    full_shape = values.shape
    split_heads = heads_of(values)
    half_size = HEAD // 2
    first_half = split_heads[..., :half_size]
    second_half = split_heads[..., half_size:]
    cosines = cosine_table[..., None, :]
    sines_now = sine_table[..., None, :] * turn_sign
    turned = jnp.concatenate(
        [
            first_half * cosines - second_half * sines_now,
            first_half * sines_now + second_half * cosines,
        ],
        axis=-1,
    )
    return turned.reshape(full_shape)


def gelu_tanh(values):
    return (
        0.5 * values * (1.0 + jnp.tanh(gelu_coef * (values + 0.044715 * values * values * values)))
    )


def gelu_slope(values):
    tangent = jnp.tanh(gelu_coef * (values + 0.044715 * values * values * values))
    return 0.5 * (1.0 + tangent) + 0.5 * values * (1.0 - tangent * tangent) * gelu_coef * (
        1.0 + 3.0 * 0.044715 * values * values
    )


def normalize(values):
    inv_rms = lax.rsqrt(jnp.mean(values * values, axis=-1, keepdims=True) + norm_eps)
    return (values * inv_rms, inv_rms)


def norm_back(grad_in, normed, inv_rms, gain):
    grad_normed = grad_in * gain
    grad_values = inv_rms * (
        grad_normed - normed * jnp.mean(grad_normed * normed, axis=-1, keepdims=True)
    )
    grad_gain = jnp.sum(grad_in * normed, axis=(0, 1))
    return (grad_values, grad_gain)


def group_rows(rows):
    seq_count, tok_count, width = rows.shape
    pad_front = jnp.zeros((seq_count, 1, width), rows.dtype)
    pad_back = jnp.zeros((seq_count, SPAN - 1, width), rows.dtype)
    joined = jnp.concatenate([pad_front, rows, pad_back], axis=1)
    return heads_of(joined.reshape(seq_count, (tok_count + SPAN) // SPAN, SPAN, width))


def ungroup(grouped, tok_count):
    flattened = grouped.reshape(grouped.shape[0], -1, HEADS * HEAD)
    return flattened[:, 1 : tok_count + 1]


def cross_mix(query_groups, key_groups, value_groups):
    probs = jax.nn.softmax(
        jnp.einsum(
            "sgqhd,sgrhd->sghqr",
            query_groups,
            heads_of(key_groups),
            preferred_element_type=jnp.float32,
        )
        * score_scale,
        axis=-1,
    )
    mixed = jnp.einsum(
        "sghqr,sgrhd->sgqhd",
        probs.astype(jnp.bfloat16),
        heads_of(value_groups),
        preferred_element_type=jnp.float32,
    )
    return (probs, mixed)


def self_probs(query_rows, all_keys, start_rows, position):
    key_index = jnp.arange(all_keys.shape[0], dtype=jnp.int32)
    scores = (
        jnp.einsum(
            "qhd,khd->hqk",
            heads_of(query_rows),
            heads_of(all_keys),
            preferred_element_type=jnp.float32,
        )
        * score_scale
    )
    allowed = (key_index[None, :] >= start_rows[:, None]) & (
        key_index[None, :] <= position[:, None]
    )
    scores = jnp.where(allowed[None], scores, -1e30)
    return jax.nn.softmax(scores, axis=-1)


def forward(qkv_shard, out_shard, in_shard, down_shard, gains, tokens, doc_start, neighbours):
    qkv_full, out_full, in_full, down_full = (
        lax.all_gather(qkv_shard, ("seq", "batch"), axis=1, tiled=True),
        lax.all_gather(out_shard, ("seq", "batch"), axis=1, tiled=True),
        lax.all_gather(in_shard, ("seq", "batch"), axis=1, tiled=True),
        lax.all_gather(down_shard, ("seq", "batch"), axis=0, tiled=True),
    )
    seq_count, tok_count, model_width = tokens.shape
    att_width = HEADS * HEAD
    position = lax.axis_index("seq") * tok_count + jnp.arange(tok_count, dtype=jnp.int32)
    cosine_table, sine_table = rope_tables((position[None, :] - doc_start).astype(jnp.float32))
    resid_in = tokens.astype(jnp.float32)
    norm_one, inv_one = normalize(resid_in)
    input_one = (norm_one * gains[0]).astype(jnp.bfloat16)
    proj_self = jnp.einsum(
        "std,de->ste", input_one, qkv_full[:, : 3 * att_width], preferred_element_type=jnp.float32
    )
    query_rot = rotate(proj_self[..., :att_width], cosine_table, sine_table, 1.0).astype(
        jnp.bfloat16
    )
    key_rot = rotate(
        proj_self[..., att_width : 2 * att_width], cosine_table, sine_table, 1.0
    ).astype(jnp.bfloat16)
    value_self = proj_self[..., 2 * att_width :].astype(jnp.bfloat16)

    def attend(carried, step_inputs):
        query_rows, key_rows, value_rows, start_rows = step_inputs
        all_keys, all_values = (
            lax.all_gather(key_rows, "seq", axis=0, tiled=True),
            lax.all_gather(value_rows, "seq", axis=0, tiled=True),
        )
        attn_probs = self_probs(query_rows, all_keys, start_rows, position)
        mixed_rows = jnp.einsum(
            "hqk,khd->qhd",
            attn_probs.astype(jnp.bfloat16),
            heads_of(all_values),
            preferred_element_type=jnp.float32,
        )
        return (
            carried,
            (mixed_rows.reshape(query_rows.shape).astype(jnp.bfloat16), all_keys, all_values),
        )

    _, (attn_self, gathered_keys, gathered_values) = lax.scan(
        attend, jnp.zeros((), jnp.int32), (query_rot, key_rot, value_self, doc_start)
    )
    resid_mid = resid_in + jnp.einsum(
        "ste,ed->std", attn_self, out_full[:, :model_width], preferred_element_type=jnp.float32
    )
    norm_two, inv_two = normalize(resid_mid)
    input_two = (norm_two * gains[1]).astype(jnp.bfloat16)
    query_cross = jnp.einsum(
        "std,de->ste",
        input_two,
        qkv_full[:, 3 * att_width : 4 * att_width],
        preferred_element_type=jnp.float32,
    ).astype(jnp.bfloat16)
    proj_cross = jnp.einsum(
        "scrd,de->scre",
        neighbours,
        qkv_full[:, 4 * att_width :],
        preferred_element_type=jnp.float32,
    )
    key_cross = proj_cross[..., :att_width].astype(jnp.bfloat16)
    value_cross = proj_cross[..., att_width:].astype(jnp.bfloat16)
    query_groups = group_rows(query_cross)
    prior_key, prior_value = passed_along((key_cross[:, -1], value_cross[:, -1]), "seq", 1)
    ext_keys = jnp.concatenate([prior_key[:, None], key_cross], axis=1)
    ext_values = jnp.concatenate([prior_value[:, None], value_cross], axis=1)
    probs_cross, mixed_groups = cross_mix(query_groups, ext_keys, ext_values)
    mixed_cross = ungroup(mixed_groups, tok_count)
    span_of = (position + 1) // SPAN - 1
    valid_rows = (
        (span_of[None, :] >= 0) & (doc_start <= span_of[None, :] * SPAN + SPAN - 1)
    ).astype(jnp.float32)
    attn_cross = (mixed_cross * valid_rows[..., None]).astype(jnp.bfloat16)
    resid_late = resid_mid + jnp.einsum(
        "ste,ed->std", attn_cross, out_full[:, model_width:], preferred_element_type=jnp.float32
    )
    norm_three, inv_three = normalize(resid_late)
    input_three = (norm_three * gains[2]).astype(jnp.bfloat16)
    pre_act = jnp.einsum("std,df->stf", input_three, in_full, preferred_element_type=jnp.float32)
    activated = gelu_tanh(pre_act).astype(jnp.bfloat16)
    result = resid_late + jnp.einsum(
        "stf,fd->std", activated, down_full, preferred_element_type=jnp.float32
    )
    kept_state = dict(
        qkv_full=qkv_full,
        out_full=out_full,
        in_full=in_full,
        down_full=down_full,
        position=position,
        cosine_table=cosine_table,
        sine_table=sine_table,
        norm_one=norm_one,
        inv_one=inv_one,
        input_one=input_one,
        query_rot=query_rot,
        attn_self=attn_self,
        gathered_keys=gathered_keys,
        gathered_values=gathered_values,
        norm_two=norm_two,
        inv_two=inv_two,
        input_two=input_two,
        cross_queries=query_groups,
        ext_keys=ext_keys,
        ext_values=ext_values,
        probs_cross=probs_cross,
        valid_rows=valid_rows,
        attn_cross=attn_cross,
        norm_three=norm_three,
        inv_three=inv_three,
        input_three=input_three,
        pre_act=pre_act,
        activated=activated,
    )
    return (result, kept_state)


def backward(kept_state, gains, neighbours, doc_start, cotangent):
    qkv_full = kept_state["qkv_full"]
    out_full = kept_state["out_full"]
    in_full = kept_state["in_full"]
    down_full = kept_state["down_full"]
    position = kept_state["position"]
    tok_count = cotangent.shape[1]
    model_width = cotangent.shape[2]
    att_width = HEADS * HEAD
    grad_final = cotangent.astype(jnp.float32)
    grad_down = jnp.einsum(
        "stf,std->fd", kept_state["activated"], cotangent, preferred_element_type=jnp.float32
    )
    grad_act = jnp.einsum("std,fd->stf", cotangent, down_full, preferred_element_type=jnp.float32)
    grad_pre = (grad_act * gelu_slope(kept_state["pre_act"])).astype(jnp.bfloat16)
    grad_in = jnp.einsum(
        "std,stf->df", kept_state["input_three"], grad_pre, preferred_element_type=jnp.float32
    )
    grad_norm_three, gain_three = norm_back(
        jnp.einsum("stf,df->std", grad_pre, in_full, preferred_element_type=jnp.float32),
        kept_state["norm_three"],
        kept_state["inv_three"],
        gains[2],
    )
    grad_late = grad_final + grad_norm_three
    grad_two = grad_late.astype(jnp.bfloat16)
    grad_cross_proj = jnp.einsum(
        "ste,std->ed", kept_state["attn_cross"], grad_two, preferred_element_type=jnp.float32
    )
    grad_cross_out = jnp.einsum(
        "std,ed->ste", grad_two, out_full[:, model_width:], preferred_element_type=jnp.float32
    ).astype(jnp.bfloat16)
    masked_grad = grad_cross_out * kept_state["valid_rows"][..., None].astype(jnp.bfloat16)
    grad_groups = group_rows(masked_grad)
    cross_queries = kept_state["cross_queries"]
    probs_cross = kept_state["probs_cross"]
    grad_probs = jnp.einsum(
        "sgqhd,sgrhd->sghqr",
        grad_groups,
        heads_of(kept_state["ext_values"]),
        preferred_element_type=jnp.float32,
    )
    grad_ext_values = jnp.einsum(
        "sghqr,sgqhd->sgrhd",
        probs_cross.astype(jnp.bfloat16),
        grad_groups,
        preferred_element_type=jnp.float32,
    )
    grad_scores = (
        probs_cross * (grad_probs - jnp.sum(probs_cross * grad_probs, axis=-1, keepdims=True))
    ).astype(jnp.bfloat16)
    grad_query_groups = (
        jnp.einsum(
            "sghqr,sgrhd->sgqhd",
            grad_scores,
            heads_of(kept_state["ext_keys"]),
            preferred_element_type=jnp.float32,
        )
        * score_scale
    )
    grad_ext_keys = (
        jnp.einsum(
            "sghqr,sgqhd->sgrhd", grad_scores, cross_queries, preferred_element_type=jnp.float32
        )
        * score_scale
    )
    flat_keys = grad_ext_keys.reshape(grad_ext_keys.shape[:3] + (att_width,))
    flat_values = grad_ext_values.reshape(grad_ext_values.shape[:3] + (att_width,))
    grad_query_cross = ungroup(grad_query_groups, tok_count).astype(jnp.bfloat16)
    later_key, later_value = (
        passed_along(flat_keys[:, 0].astype(jnp.bfloat16), "seq", -1).astype(jnp.float32),
        passed_along(flat_values[:, 0].astype(jnp.bfloat16), "seq", -1).astype(jnp.float32),
    )
    own_keys = flat_keys[:, 1:].at[:, -1].add(later_key)
    own_values = flat_values[:, 1:].at[:, -1].add(later_value)
    grad_kv_cross = jnp.concatenate(
        [own_keys.astype(jnp.bfloat16), own_values.astype(jnp.bfloat16)], axis=-1
    )
    grad_neighbours = jnp.einsum(
        "scre,de->scrd",
        grad_kv_cross,
        qkv_full[:, 4 * att_width :],
        preferred_element_type=jnp.float32,
    )
    grad_cross_kv = jnp.einsum(
        "scrd,scre->de", neighbours, grad_kv_cross, preferred_element_type=jnp.float32
    )
    grad_cross_q = jnp.einsum(
        "std,ste->de", kept_state["input_two"], grad_query_cross, preferred_element_type=jnp.float32
    )
    grad_norm_two, gain_two = norm_back(
        jnp.einsum(
            "ste,de->std",
            grad_query_cross,
            qkv_full[:, 3 * att_width : 4 * att_width],
            preferred_element_type=jnp.float32,
        ),
        kept_state["norm_two"],
        kept_state["inv_two"],
        gains[1],
    )
    grad_mid = grad_late + grad_norm_two
    grad_one = grad_mid.astype(jnp.bfloat16)
    grad_self_proj = jnp.einsum(
        "ste,std->ed", kept_state["attn_self"], grad_one, preferred_element_type=jnp.float32
    )
    grad_attn_self = jnp.einsum(
        "std,ed->ste", grad_one, out_full[:, :model_width], preferred_element_type=jnp.float32
    ).astype(jnp.bfloat16)

    def attend_back(carried, step_inputs):
        query_rows, grad_rows, all_keys, all_values, start_rows = step_inputs
        attn_probs = self_probs(query_rows, all_keys, start_rows, position)
        grad_attn = jnp.einsum(
            "qhd,khd->hqk",
            heads_of(grad_rows),
            heads_of(all_values),
            preferred_element_type=jnp.float32,
        )
        grad_vals = jnp.einsum(
            "hqk,qhd->khd",
            attn_probs.astype(jnp.bfloat16),
            heads_of(grad_rows),
            preferred_element_type=jnp.float32,
        )
        grad_logits = (
            attn_probs * (grad_attn - jnp.sum(attn_probs * grad_attn, axis=-1, keepdims=True))
        ).astype(jnp.bfloat16)
        grad_query = (
            jnp.einsum(
                "hqk,khd->qhd", grad_logits, heads_of(all_keys), preferred_element_type=jnp.float32
            )
            * score_scale
        )
        grad_keys = (
            jnp.einsum(
                "hqk,qhd->khd",
                grad_logits,
                heads_of(query_rows),
                preferred_element_type=jnp.float32,
            )
            * score_scale
        )
        own_key_grad, own_value_grad = (
            lax.psum_scatter(
                grad_keys.reshape(all_keys.shape).astype(jnp.bfloat16),
                "seq",
                scatter_dimension=0,
                tiled=True,
            ).astype(jnp.float32),
            lax.psum_scatter(
                grad_vals.reshape(all_values.shape).astype(jnp.bfloat16),
                "seq",
                scatter_dimension=0,
                tiled=True,
            ).astype(jnp.float32),
        )
        return (carried, (grad_query.reshape(query_rows.shape), own_key_grad, own_value_grad))

    _, (grad_query_rot, grad_key_rot, grad_value_rows) = lax.scan(
        attend_back,
        jnp.zeros((), jnp.int32),
        (
            kept_state["query_rot"],
            grad_attn_self,
            kept_state["gathered_keys"],
            kept_state["gathered_values"],
            doc_start,
        ),
    )
    cosine_table = kept_state["cosine_table"]
    sine_table = kept_state["sine_table"]
    grad_query_lin = rotate(grad_query_rot, cosine_table, sine_table, -1.0).astype(jnp.bfloat16)
    grad_key_lin = rotate(grad_key_rot, cosine_table, sine_table, -1.0).astype(jnp.bfloat16)
    grad_value_lin = grad_value_rows.astype(jnp.bfloat16)
    grad_lin = jnp.concatenate([grad_query_lin, grad_key_lin, grad_value_lin], axis=-1)
    grad_self_qkv = jnp.einsum(
        "std,ste->de", kept_state["input_one"], grad_lin, preferred_element_type=jnp.float32
    )
    grad_norm_one, gain_one = norm_back(
        jnp.einsum(
            "ste,de->std",
            grad_lin,
            qkv_full[:, : 3 * att_width],
            preferred_element_type=jnp.float32,
        ),
        kept_state["norm_one"],
        kept_state["inv_one"],
        gains[0],
    )
    grad_tokens = grad_mid + grad_norm_one
    grad_qkv_full = jnp.concatenate([grad_self_qkv, grad_cross_q, grad_cross_kv], axis=1)
    grad_out_full = jnp.concatenate([grad_self_proj, grad_cross_proj], axis=1)
    shard_qkv, shard_out, shard_in, shard_down = (
        lax.psum_scatter(grad_qkv_full, ("seq", "batch"), scatter_dimension=1, tiled=True),
        lax.psum_scatter(grad_out_full, ("seq", "batch"), scatter_dimension=1, tiled=True),
        lax.psum_scatter(grad_in, ("seq", "batch"), scatter_dimension=1, tiled=True),
        lax.psum_scatter(grad_down, ("seq", "batch"), scatter_dimension=0, tiled=True),
    )
    grad_gains = lax.psum(jnp.stack([gain_one, gain_two, gain_three]), ("seq", "batch"))
    return (grad_tokens, grad_neighbours, shard_qkv, shard_out, shard_in, shard_down, grad_gains)


def on_device(
    tokens, doc_start, neighbours, qkv_weight, out_weight, ff_in, ff_out, gains, cotangent
):
    result, kept_state = forward(
        qkv_weight, out_weight, ff_in, ff_out, gains, tokens, doc_start, neighbours
    )
    output = result.astype(jnp.bfloat16)
    fenced = lax.optimization_barrier(
        (qkv_weight, out_weight, ff_in, ff_out, tokens, neighbours, output)
    )
    _, kept_state = forward(
        fenced[0], fenced[1], fenced[2], fenced[3], gains, fenced[4], doc_start, fenced[5]
    )
    grads = backward(kept_state, gains, neighbours, doc_start, cotangent)
    return (output,) + grads


def solution(mesh):
    placed = (
        P("batch", "seq", None),
        P("batch", "seq"),
        P("batch", "seq", None, None),
        P(None, ("seq", "batch")),
        P(None, ("seq", "batch")),
        P(None, ("seq", "batch")),
        P(("seq", "batch"), None),
        P(),
        P("batch", "seq", None),
    )
    return jax.shard_map(
        on_device,
        mesh=mesh,
        in_specs=placed,
        out_specs=(
            P("batch", "seq", None),
            P("batch", "seq", None),
            P("batch", "seq", None, None),
            P(None, ("seq", "batch")),
            P(None, ("seq", "batch")),
            P(None, ("seq", "batch")),
            P(("seq", "batch"), None),
            P(),
        ),
        check_vma=False,
    )
```

profile of v0, /device:TPU:0, one launch (start us, length us, event | category | flops | bytes accessed | tf_op | source)
XLA Modules:
  0.0 3013.9 jit_solution(10323187282839341883)
XLA Ops:
  12.5 90.1 %all-gather.29.cloned.1.call-done = bf16[896,6144]{0,1:T(8,128)(2,1)} async-done(((bf16[896,192]{0,1:T(8,128)(2,1)}), bf16[896,6144]{0,1:T(8,128)(2,1)}) %all-gather.29.cloned.1.call-update) | async-done | bytes 11010064 | tf_op jit(solution)/shard_map/all_gather | solution.py:133
  120.2 443.6 %while.43 = (s32[]{:T(128)}, bf16[4,128,1024]{1,2,0:T(8,128)(2,1)}, bf16[4,128,1024]{2,1,0:T(8,128)(2,1)S(1)}, s32[4,128]{1,0:T(4,128)S(1)}, bf16[4,128,1024]{1,...) while((s32[]{:T(128)}, bf16[4,128,1024]{1,2,0:T(8,128)(2,1)}, ...), condition=%wide.region_4.5_spmd.clone, body=%wide.region_1.4_spmd.clone.sunk | while | flops 549979264 | bytes 38554308 | solution.py:174
  123.1 50.0 %all-gather.47.cloned.1.call-done = bf16[1,1024,1024]{1,2,0:T(8,128)(2,1)} async-done(((bf16[1,128,1024]{1,2,0:T(8,128)(2,1)}), bf16[1,1024,1024]{1,2,0:T(8,128)(2,1)}) %all-gather.47.cloned.1.call-update) | async-done | bytes 2097168 | tf_op jit(solution)/shard_map/while/body/eval_jaxpr/all_gather | solution.py:159
  181.1 44.0 %all-gather.45.cloned.1.call-done = bf16[1,1024,1024]{1,2,0:T(8,128)(2,1)} async-done(((bf16[1,128,1024]{1,2,0:T(8,128)(2,1)}), bf16[1,1024,1024]{1,2,0:T(8,128)(2,1)}) %all-gather.45.cloned.1.call-update) | async-done | bytes 2097168 | tf_op jit(solution)/shard_map/while/body/eval_jaxpr/all_gather | solution.py:160
  234.4 49.5 %all-gather.47.cloned.1.call-done = bf16[1,1024,1024]{1,2,0:T(8,128)(2,1)} async-done(((bf16[1,128,1024]{1,2,0:T(8,128)(2,1)}), bf16[1,1024,1024]{1,2,0:T(8,128)(2,1)}) %all-gather.47.cloned.1.call-update) | async-done | bytes 2097168 | tf_op jit(solution)/shard_map/while/body/eval_jaxpr/all_gather | solution.py:159
  291.9 43.8 %all-gather.45.cloned.1.call-done = bf16[1,1024,1024]{1,2,0:T(8,128)(2,1)} async-done(((bf16[1,128,1024]{1,2,0:T(8,128)(2,1)}), bf16[1,1024,1024]{1,2,0:T(8,128)(2,1)}) %all-gather.45.cloned.1.call-update) | async-done | bytes 2097168 | tf_op jit(solution)/shard_map/while/body/eval_jaxpr/all_gather | solution.py:160
  345.0 49.5 %all-gather.47.cloned.1.call-done = bf16[1,1024,1024]{1,2,0:T(8,128)(2,1)} async-done(((bf16[1,128,1024]{1,2,0:T(8,128)(2,1)}), bf16[1,1024,1024]{1,2,0:T(8,128)(2,1)}) %all-gather.47.cloned.1.call-update) | async-done | bytes 2097168 | tf_op jit(solution)/shard_map/while/body/eval_jaxpr/all_gather | solution.py:159
  402.4 43.9 %all-gather.45.cloned.1.call-done = bf16[1,1024,1024]{1,2,0:T(8,128)(2,1)} async-done(((bf16[1,128,1024]{1,2,0:T(8,128)(2,1)}), bf16[1,1024,1024]{1,2,0:T(8,128)(2,1)}) %all-gather.45.cloned.1.call-update) | async-done | bytes 2097168 | tf_op jit(solution)/shard_map/while/body/eval_jaxpr/all_gather | solution.py:160
  455.7 49.8 %all-gather.47.cloned.1.call-done = bf16[1,1024,1024]{1,2,0:T(8,128)(2,1)} async-done(((bf16[1,128,1024]{1,2,0:T(8,128)(2,1)}), bf16[1,1024,1024]{1,2,0:T(8,128)(2,1)}) %all-gather.47.cloned.1.call-update) | async-done | bytes 2097168 | tf_op jit(solution)/shard_map/while/body/eval_jaxpr/all_gather | solution.py:159
  513.5 43.9 %all-gather.45.cloned.1.call-done = bf16[1,1024,1024]{1,2,0:T(8,128)(2,1)} async-done(((bf16[1,128,1024]{1,2,0:T(8,128)(2,1)}), bf16[1,1024,1024]{1,2,0:T(8,128)(2,1)}) %all-gather.45.cloned.1.call-update) | async-done | bytes 2097168 | tf_op jit(solution)/shard_map/while/body/eval_jaxpr/all_gather | solution.py:160
  746.9 48.3 %all-gather.35.cloned.1.call-done = bf16[3584,896]{1,0:T(8,128)(2,1)} async-done(((bf16[112,896]{1,0:T(8,128)(2,1)}), bf16[3584,896]{1,0:T(8,128)(2,1)}) %all-gather.35.cloned.1.call-update) | async-done | bytes 6422544 | tf_op jit(solution)/shard_map/all_gather | solution.py:136
  810.1 87.3 %all-gather.37.cloned.1.call-done = bf16[896,6144]{0,1:T(8,128)(2,1)} async-done(((bf16[896,192]{0,1:T(8,128)(2,1)}), bf16[896,6144]{0,1:T(8,128)(2,1)}) %all-gather.37.cloned.1.call-update) | async-done | bytes 11010064 | tf_op jit(solution)/shard_map/all_gather | solution.py:133
  914.7 455.8 %while.44 = (s32[]{:T(128)}, bf16[4,128,1024]{1,2,0:T(8,128)(2,1)}, bf16[4,1024,1024]{1,2,0:T(8,128)(2,1)}, bf16[4,1024,1024]{1,2,0:T(8,128)(2,1)}, bf16[4,128,1...) while((s32[]{:T(128)}, bf16[4,128,1024]{1,2,0:T(8,128)(2,1)}, ...), condition=%wide.region_13.14_spmd.clone, body=%wide.region_10.13_spmd.clone.sunk | while | flops 549979264 | bytes 63720212 | solution.py:174
  917.9 49.7 %all-gather.51.cloned.1.call-done = bf16[1,1024,1024]{1,2,0:T(8,128)(2,1)} async-done(((bf16[1,128,1024]{1,2,0:T(8,128)(2,1)}), bf16[1,1024,1024]{1,2,0:T(8,128)(2,1)}) %all-gather.51.cloned.1.call-update) | async-done | bytes 2097168 | tf_op jit(solution)/shard_map/while/body/eval_jaxpr/all_gather | solution.py:159
  1031.8 49.5 %all-gather.51.cloned.1.call-done = bf16[1,1024,1024]{1,2,0:T(8,128)(2,1)} async-done(((bf16[1,128,1024]{1,2,0:T(8,128)(2,1)}), bf16[1,1024,1024]{1,2,0:T(8,128)(2,1)}) %all-gather.51.cloned.1.call-update) | async-done | bytes 2097168 | tf_op jit(solution)/shard_map/while/body/eval_jaxpr/all_gather | solution.py:159
  1145.7 49.5 %all-gather.51.cloned.1.call-done = bf16[1,1024,1024]{1,2,0:T(8,128)(2,1)} async-done(((bf16[1,128,1024]{1,2,0:T(8,128)(2,1)}), bf16[1,1024,1024]{1,2,0:T(8,128)(2,1)}) %all-gather.51.cloned.1.call-update) | async-done | bytes 2097168 | tf_op jit(solution)/shard_map/while/body/eval_jaxpr/all_gather | solution.py:159
  1203.3 43.8 %all-gather.49.cloned.1.call-done = bf16[1,1024,1024]{1,2,0:T(8,128)(2,1)} async-done(((bf16[1,128,1024]{1,2,0:T(8,128)(2,1)}), bf16[1,1024,1024]{1,2,0:T(8,128)(2,1)}) %all-gather.49.cloned.1.call-update) | async-done | bytes 2097168 | tf_op jit(solution)/shard_map/while/body/eval_jaxpr/all_gather | solution.py:160
  1259.5 49.5 %all-gather.51.cloned.1.call-done = bf16[1,1024,1024]{1,2,0:T(8,128)(2,1)} async-done(((bf16[1,128,1024]{1,2,0:T(8,128)(2,1)}), bf16[1,1024,1024]{1,2,0:T(8,128)(2,1)}) %all-gather.51.cloned.1.call-update) | async-done | bytes 2097168 | tf_op jit(solution)/shard_map/while/body/eval_jaxpr/all_gather | solution.py:159
  1317.1 43.8 %all-gather.49.cloned.1.call-done = bf16[1,1024,1024]{1,2,0:T(8,128)(2,1)} async-done(((bf16[1,128,1024]{1,2,0:T(8,128)(2,1)}), bf16[1,1024,1024]{1,2,0:T(8,128)(2,1)}) %all-gather.49.cloned.1.call-update) | async-done | bytes 2097168 | tf_op jit(solution)/shard_map/while/body/eval_jaxpr/all_gather | solution.py:160
  1686.6 630.7 %while.45 = (s32[]{:T(128)}, f32[4,128,1024]{1,2,0:T(8,128)}, f32[4,128,1024]{1,2,0:T(8,128)}, bf16[4,128,1024]{2,1,0:T(8,128)(2,1)}, bf16[4,1024,1024]{1,2,0:T(...) while((s32[]{:T(128)}, f32[4,128,1024]{1,2,0:T(8,128)}, ...), condition=%wide.region_27.28_spmd.clone, body=%wide.region_21.27_spmd.clone.sunk | while | flops 1373240448 | bytes 170445712 | solution.py:409
  1724.5 47.5 %reduce-scatter.27.cloned.1.call-done = bf16[128,1024]{1,0:T(8,128)(2,1)} async-done(((bf16[1024,1024]{1,0:T(8,128)(2,1)}), bf16[128,1024]{1,0:T(8,128)(2,1)}) %reduce-scatter.27.cloned.1.call-update) | async-done | bytes 262160 | tf_op jit(solution)/shard_map/while
  1774.0 68.3 %reduce-scatter.25.cloned.1.call-done = bf16[128,1024]{1,0:T(8,128)(2,1)} async-done(((bf16[1024,1024]{1,0:T(8,128)(2,1)}), bf16[128,1024]{1,0:T(8,128)(2,1)}) %reduce-scatter.25.cloned.1.call-update) | async-done | bytes 262160 | tf_op jit(solution)/shard_map/while
  1881.6 48.2 %reduce-scatter.27.cloned.1.call-done = bf16[128,1024]{1,0:T(8,128)(2,1)} async-done(((bf16[1024,1024]{1,0:T(8,128)(2,1)}), bf16[128,1024]{1,0:T(8,128)(2,1)}) %reduce-scatter.27.cloned.1.call-update) | async-done | bytes 262160 | tf_op jit(solution)/shard_map/while
  1931.8 68.1 %reduce-scatter.25.cloned.1.call-done = bf16[128,1024]{1,0:T(8,128)(2,1)} async-done(((bf16[1024,1024]{1,0:T(8,128)(2,1)}), bf16[128,1024]{1,0:T(8,128)(2,1)}) %reduce-scatter.25.cloned.1.call-update) | async-done | bytes 262160 | tf_op jit(solution)/shard_map/while
  2039.3 48.2 %reduce-scatter.27.cloned.1.call-done = bf16[128,1024]{1,0:T(8,128)(2,1)} async-done(((bf16[1024,1024]{1,0:T(8,128)(2,1)}), bf16[128,1024]{1,0:T(8,128)(2,1)}) %reduce-scatter.27.cloned.1.call-update) | async-done | bytes 262160 | tf_op jit(solution)/shard_map/while
  2089.4 68.1 %reduce-scatter.25.cloned.1.call-done = bf16[128,1024]{1,0:T(8,128)(2,1)} async-done(((bf16[1024,1024]{1,0:T(8,128)(2,1)}), bf16[128,1024]{1,0:T(8,128)(2,1)}) %reduce-scatter.25.cloned.1.call-update) | async-done | bytes 262160 | tf_op jit(solution)/shard_map/while
  2196.9 48.2 %reduce-scatter.27.cloned.1.call-done = bf16[128,1024]{1,0:T(8,128)(2,1)} async-done(((bf16[1024,1024]{1,0:T(8,128)(2,1)}), bf16[128,1024]{1,0:T(8,128)(2,1)}) %reduce-scatter.27.cloned.1.call-update) | async-done | bytes 262160 | tf_op jit(solution)/shard_map/while
  2247.1 68.2 %reduce-scatter.25.cloned.1.call-done = bf16[128,1024]{1,0:T(8,128)(2,1)} async-done(((bf16[1024,1024]{1,0:T(8,128)(2,1)}), bf16[128,1024]{1,0:T(8,128)(2,1)}) %reduce-scatter.25.cloned.1.call-update) | async-done | bytes 262160 | tf_op jit(solution)/shard_map/while
  2431.6 51.4 %collective-permute-done.5 = bf16[4,256,1024]{2,1,0:T(8,128)(2,1)} collective-permute-done((bf16[4,256,1024]{2,1,0:T(8,128)(2,1)}, bf16[4,256,1024]{2,1,0:T(8,128)(2,1)}, u32[]{:S(2)}, u32[]{:S(2)}) %collective-permute-start.5) | collective-permute-done | bytes 2097184 | tf_op jit(solution)/shard_map/ppermute | solution.py:21
  2547.9 52.9 %psum.7 = f32[3,896]{1,0:T(4,128)} all-reduce(f32[3,896]{1,0:T(4,128)S(1)} %pad_maximum_fusion.22), channel_id=1, replica_groups=mesh['seq'=8,'batch'=4] {'seq','batch'}, use_global_device_ids=true, to_apply=%region_36.37 | all-reduce | flops 2688 | bytes 21504 | tf_op jit(solution)/shard_map/psum | solution.py:449
  2623.1 156.5 %reduce-scatter.19.cloned.1.call-done = f32[896,112]{0,1:T(8,128)} async-done(((f32[896,3584]{0,1:T(8,128)}), f32[896,112]{0,1:T(8,128)}) %reduce-scatter.19.cloned.1.call-update) | async-done | bytes 401424 | tf_op jit(solution)/shard_map/reduce_scatter | solution.py:446
  2779.6 227.3 %reduce-scatter.23.cloned.1.call-done = f32[192,896]{1,0:T(8,128)} async-done(((f32[6144,896]{1,0:T(8,128)}), f32[192,896]{1,0:T(8,128)}) %reduce-scatter.23.cloned.1.call-update) | async-done | bytes 688144
  (619 shorter events, 1158.0 us)
Async XLA Ops:
  7.2 95.4 %all-gather.29.cloned.1.call-start = ((), (), s32[]{:S(2)}) async-start(), calls=%async_computation.6 | async-start | bytes 11354112 | tf_op jit(solution)/shard_map/all_gather | solution.py:133
  121.0 104.1 %all-gather.45.cloned.1.call-start = ((), (), s32[]{:S(2)}) async-start(), calls=%async_computation.18 | async-start | bytes 2359296 | tf_op jit(solution)/shard_map/while/body/eval_jaxpr/all_gather | solution.py:160
  232.2 103.4 %all-gather.45.cloned.1.call-start = ((), (), s32[]{:S(2)}) async-start(), calls=%async_computation.18 | async-start | bytes 2359296 | tf_op jit(solution)/shard_map/while/body/eval_jaxpr/all_gather | solution.py:160
  342.8 103.6 %all-gather.45.cloned.1.call-start = ((), (), s32[]{:S(2)}) async-start(), calls=%async_computation.18 | async-start | bytes 2359296 | tf_op jit(solution)/shard_map/while/body/eval_jaxpr/all_gather | solution.py:160
  453.5 103.9 %all-gather.45.cloned.1.call-start = ((), (), s32[]{:S(2)}) async-start(), calls=%async_computation.18 | async-start | bytes 2359296 | tf_op jit(solution)/shard_map/while/body/eval_jaxpr/all_gather | solution.py:160
  564.4 182.5 %all-gather.33.cloned.1.call-start = ((), (), s32[]{:S(2)}) async-start(), calls=%async_computation.8 | async-start | bytes 6623232 | tf_op jit(solution)/shard_map/all_gather | solution.py:135
  565.1 230.1 %all-gather.35.cloned.1.call-start = ((), (), s32[]{:S(2)}) async-start(), calls=%async_computation.9 | async-start | bytes 6623232 | tf_op jit(solution)/shard_map/all_gather | solution.py:136
  565.7 331.6 %all-gather.37.cloned.1.call-start = ((), (), s32[]{:S(2)}) async-start(), calls=%async_computation.10 | async-start | bytes 11354112 | tf_op jit(solution)/shard_map/all_gather | solution.py:133
  582.6 79.3 %collective-permute-start = (bf16[4,256,1024]{2,1,0:T(8,128)(2,1)}, bf16[4,256,1024]{2,1,0:T(8,128)(2,1)}, u32[]{:S(2)}, u32[]{:S(2)}) collective-permute-start(bf16[4,256,1024]{2,1,0:T(8,128)(2,1)} %get-tuple-element.431), channel_id=1, source_target_pairs={{0,4},{4,8},{8,12},{12,16},{16,20},{20,24},{24,28},{1,5},{5,9},{9,... | collective-permute-start | bytes 6291464 | tf_op jit(solution)/shard_map/ppermute | solution.py:21
  587.3 103.8 %collective-permute-start.1 = (bf16[4,256,1024]{2,1,0:T(8,128)(2,1)}, bf16[4,256,1024]{2,1,0:T(8,128)(2,1)}, u32[]{:S(2)}, u32[]{:S(2)}) collective-permute-start(bf16[4,256,1024]{2,1,0:T(8,128)(2,1)} %get-tuple-element.432), channel_id=1, source_target_pairs={{0,4},{4,8},{8,12},{12,16},{16,20},{20,24},{24,28},{1,5},{5,9},{9,... | collective-permute-start | bytes 6291464 | tf_op jit(solution)/shard_map/ppermute | solution.py:21
  915.8 103.6 %all-gather.49.cloned.1.call-start = ((), (), s32[]{:S(2)}) async-start(), calls=%async_computation.20 | async-start | bytes 2359296 | tf_op jit(solution)/shard_map/while/body/eval_jaxpr/all_gather | solution.py:160
  1029.6 103.4 %all-gather.49.cloned.1.call-start = ((), (), s32[]{:S(2)}) async-start(), calls=%async_computation.20 | async-start | bytes 2359296 | tf_op jit(solution)/shard_map/while/body/eval_jaxpr/all_gather | solution.py:160
  1143.5 103.6 %all-gather.49.cloned.1.call-start = ((), (), s32[]{:S(2)}) async-start(), calls=%async_computation.20 | async-start | bytes 2359296 | tf_op jit(solution)/shard_map/while/body/eval_jaxpr/all_gather | solution.py:160
  1257.4 103.6 %all-gather.49.cloned.1.call-start = ((), (), s32[]{:S(2)}) async-start(), calls=%async_computation.20 | async-start | bytes 2359296 | tf_op jit(solution)/shard_map/while/body/eval_jaxpr/all_gather | solution.py:160
  1370.5 69.1 %all-gather.39.cloned.1.call-start = ((), (), s32[]{:S(2)}) async-start(), calls=%async_computation.11 | async-start | bytes 3784704 | tf_op jit(solution)/shard_map/all_gather | solution.py:134
  1371.2 180.9 %all-gather.43.cloned.1.call-start = ((), (), s32[]{:S(2)}) async-start(), calls=%async_computation.13 | async-start | bytes 6623232 | tf_op jit(solution)/shard_map/all_gather | solution.py:135
  1372.0 229.6 %all-gather.41.cloned.1.call-start = ((), (), s32[]{:S(2)}) async-start(), calls=%async_computation.12 | async-start | bytes 6623232 | tf_op jit(solution)/shard_map/all_gather | solution.py:136
  1393.6 103.1 %collective-permute-start.2 = (bf16[4,256,1024]{2,1,0:T(8,128)(2,1)}, bf16[4,256,1024]{2,1,0:T(8,128)(2,1)}, u32[]{:S(2)}, u32[]{:S(2)}) collective-permute-start(bf16[4,256,1024]{2,1,0:T(8,128)(2,1)} %get-tuple-element.428), channel_id=1, source_target_pairs={{0,4},{4,8},{8,12},{12,16},{16,20},{20,24},{24,28},{1,5},{5,9},{9,... | collective-permute-start | bytes 6291464 | tf_op jit(solution)/shard_map/ppermute | solution.py:21
  1687.1 85.0 %reduce-scatter.27.cloned.1.call-start = ((), (), s32[]{:S(2)}) async-start(), calls=%async_computation.23 | async-start | bytes 2359296 | tf_op jit(solution)/shard_map/while
  1705.8 136.5 %reduce-scatter.25.cloned.1.call-start = ((), (), s32[]{:S(2)}) async-start(), calls=%async_computation.22 | async-start | bytes 2359296 | tf_op jit(solution)/shard_map/while
  1844.3 85.6 %reduce-scatter.27.cloned.1.call-start = ((), (), s32[]{:S(2)}) async-start(), calls=%async_computation.23 | async-start | bytes 2359296 | tf_op jit(solution)/shard_map/while
  1863.0 137.0 %reduce-scatter.25.cloned.1.call-start = ((), (), s32[]{:S(2)}) async-start(), calls=%async_computation.22 | async-start | bytes 2359296 | tf_op jit(solution)/shard_map/while
  2001.9 85.5 %reduce-scatter.27.cloned.1.call-start = ((), (), s32[]{:S(2)}) async-start(), calls=%async_computation.23 | async-start | bytes 2359296 | tf_op jit(solution)/shard_map/while
  2020.7 136.8 %reduce-scatter.25.cloned.1.call-start = ((), (), s32[]{:S(2)}) async-start(), calls=%async_computation.22 | async-start | bytes 2359296 | tf_op jit(solution)/shard_map/while
  2159.5 85.6 %reduce-scatter.27.cloned.1.call-start = ((), (), s32[]{:S(2)}) async-start(), calls=%async_computation.23 | async-start | bytes 2359296 | tf_op jit(solution)/shard_map/while
  2178.2 137.0 %reduce-scatter.25.cloned.1.call-start = ((), (), s32[]{:S(2)}) async-start(), calls=%async_computation.22 | async-start | bytes 2359296 | tf_op jit(solution)/shard_map/while
  2317.2 300.5 %reduce-scatter.17.cloned.1.call-start = ((), (), s32[]{:S(2)}) async-start(), calls=%async_computation.14 | async-start | bytes 7569408 | tf_op jit(solution)/shard_map/reduce_scatter | solution.py:445
  2317.8 305.3 %reduce-scatter.21.cloned.1.call-start = ((), (), s32[]{:S(2)}) async-start(), calls=%async_computation.16 | async-start | bytes 13246464 | tf_op jit(solution)/shard_map/reduce_scatter | solution.py:447
  2331.1 448.4 %reduce-scatter.19.cloned.1.call-start = ((), (), s32[]{:S(2)}) async-start(), calls=%async_computation.15 | async-start | bytes 13246464 | tf_op jit(solution)/shard_map/reduce_scatter | solution.py:446
  2341.6 665.3 %reduce-scatter.23.cloned.1.call-start = ((), (), s32[]{:S(2)}) async-start(), calls=%async_computation.17 | async-start | bytes 22708224
  2355.4 71.1 %collective-permute-start.4 = (bf16[4,256,1024]{2,1,0:T(8,128)(2,1)}, bf16[4,256,1024]{2,1,0:T(8,128)(2,1)}, u32[]{:S(2)}, u32[]{:S(2)}) collective-permute-start(bf16[4,256,1024]{2,1,0:T(8,128)(2,1)} %bitcast.378), channel_id=1, source_target_pairs={{4,0},{8,4},{12,8},{16,12},{20,16},{24,20},{28,24},{5,1},{9,5},{13... | collective-permute-start | bytes 6291464 | tf_op jit(solution)/shard_map/ppermute | solution.py:21
  2370.8 112.2 %collective-permute-start.5 = (bf16[4,256,1024]{2,1,0:T(8,128)(2,1)}, bf16[4,256,1024]{2,1,0:T(8,128)(2,1)}, u32[]{:S(2)}, u32[]{:S(2)}) collective-permute-start(bf16[4,256,1024]{2,1,0:T(8,128)(2,1)} %bitcast.381), channel_id=1, source_target_pairs={{4,0},{8,4},{12,8},{16,12},{20,16},{24,20},{28,24},{5,1},{9,5},{13... | collective-permute-start | bytes 6291464 | tf_op jit(solution)/shard_map/ppermute | solution.py:21
  (118 other events, 3732.8 us)
Sparse Core Ops, SparseCore 0:
  10.9 91.6 all-gather.28
  123.7 49.4 all-gather.46
  175.8 49.2 all-gather.44
  234.6 49.2 all-gather.46
  286.4 49.2 all-gather.44
  345.2 49.2 all-gather.46
  397.1 49.2 all-gather.44
  508.1 49.2 all-gather.44
  567.2 65.4 all-gather.30
  635.5 85.6 all-gather.32
  723.9 71.2 all-gather.34
  809.9 87.4 all-gather.36
  918.1 49.4 all-gather.50
  970.1 49.2 all-gather.48
  1083.8 49.2 all-gather.48
  1197.8 49.2 all-gather.48
  1311.7 49.2 all-gather.48
  1374.2 65.4 all-gather.38
  1442.5 85.6 all-gather.42
  1530.9 70.5 all-gather.40
  1705.9 66.0 reduce-scatter.26
  1775.4 66.8 reduce-scatter.24
  1863.1 66.6 reduce-scatter.26
  1933.3 66.5 reduce-scatter.24
  2020.8 66.6 reduce-scatter.26
  2090.8 66.6 reduce-scatter.24
  2178.3 66.6 reduce-scatter.26
  2248.6 66.6 reduce-scatter.24
  2320.6 146.2 reduce-scatter.16
  2469.8 153.2 reduce-scatter.20
  2626.0 153.5 reduce-scatter.18
  2786.4 220.4 reduce-scatter.22
  (4 shorter events, 196.8 us)
where the time goes:
time: 3020 us; the launch traced here: 3010 us
  waiting for transfers between devices  2050 us (68%)
  matrix products  436 us (14%)
  local copies, waits for them, and re-layouts  334 us (11%)
  other arithmetic  103 us (3%)
  blocking collectives  52.9 us (2%)
    while x32, waiting for transfers between devices  465 us
    all_gather x8, waiting for transfers between devices, attend(): lax.all_gather(key_rows, 'seq', axis=0, tiled=True)  397 us
    all_gather x8, waiting for transfers between devices, attend(): lax.all_gather(value_rows, 'seq', axis=0, tiled=True)  351 us
    unnamed x13, waiting for transfers between devices  232 us
    all_gather x2, waiting for transfers between devices, forward(): lax.all_gather(qkv_shard, ('seq', 'batch'), axis=1, tiled=True)  177 us
    reduce_scatter x1, waiting for transfers between devices, backward(): lax.psum_scatter(grad_in, ('seq', 'batch'), scatter_dimension=1, tiled=True)  156 us
    ppermute x6, waiting for transfers between devices, passed_along(): lax.ppermute(value, axis, [(source, source + steps) for source in range(l...  114 us
    all_gather x2, waiting for transfers between devices, forward(): lax.all_gather(down_shard, ('seq', 'batch'), axis=0, tiled=True)  87.2 us
  transfers between devices with their start and end apart: 42, of which 36 were waited for; matrix products, arithmetic and copies ran while one was open for 18% of the time, Pallas kernels for 0%

commit v1 on v0

v1 whole, which is shorter than its diff:
```python
import functools
import math

import jax
import jax.numpy as jnp
from jax import lax
from jax.experimental import pallas as pl
from jax.experimental.pallas import tpu as pltpu
from jax.sharding import PartitionSpec as P

HEADS = 16
HEAD = 64
SPAN = 64
ATT = HEADS * HEAD
SHIFT = SPAN - 1
BOTH = ("seq", "batch")

score_scale = 0.125
gelu_coef = math.sqrt(2.0 / math.pi)
norm_eps = 1e-05
BF = jnp.bfloat16
F32 = jnp.float32

NT = (((1,), (1,)), ((), ()))
NN = (((1,), (0,)), ((), ()))
TN = (((0,), (0,)), ((), ()))


def mm(left, right, dims):
    return lax.dot_general(left, right, dims, preferred_element_type=F32)


def params(**kw):
    return pltpu.CompilerParams(vmem_limit_bytes=60 * 1024 * 1024, **kw)


def cost(flops, size, exps=0):
    return pl.CostEstimate(flops=int(flops), bytes_accessed=int(size), transcendentals=int(exps))


def half_swap(values):
    width = values.shape[-1]
    half = HEAD // 2
    lane = lax.broadcasted_iota(jnp.int32, values.shape, 1)
    if width % 128 == 0:
        ahead = pltpu.roll(values, width - half, 1)
        behind = pltpu.roll(values, half, 1)
    else:
        ahead = jnp.concatenate([values[:, half:], values[:, :half]], axis=1)
        behind = jnp.concatenate([values[:, -half:], values[:, :-half]], axis=1)
    return jnp.where(lane % HEAD < half, ahead, behind)


def proj_kernel(x_ref, wq_ref, wk_ref, wv_ref, cos_ref, sin_ref, out_ref):
    groups, _, width3 = out_ref.shape
    width = width3 // 3
    x = x_ref[...]
    for part, w_ref in enumerate((wq_ref, wk_ref, wv_ref)):
        acc = mm(x, w_ref[...], NT)
        for g in range(groups):
            piece = acc[:, g * width : (g + 1) * width]
            if part < 2:
                piece = piece * cos_ref[...] + half_swap(piece) * sin_ref[...]
            out_ref[g, :, part * width : (part + 1) * width] = piece.astype(BF)


def project_self(x, qkv_t, cos_rows, sin_rows, parts):
    rows, model = x.shape
    width = ATT // parts
    groups = 2 if width % 128 == 0 else 1
    steps = parts // groups
    wide = groups * width
    full = lambda i: (0, 0)
    return pl.pallas_call(
        proj_kernel,
        grid=(steps,),
        in_specs=[
            pl.BlockSpec((rows, model), full),
            pl.BlockSpec((wide, model), lambda i: (i, 0)),
            pl.BlockSpec((wide, model), lambda i: (steps + i, 0)),
            pl.BlockSpec((wide, model), lambda i: (2 * steps + i, 0)),
            pl.BlockSpec((rows, width), full),
            pl.BlockSpec((rows, width), full),
        ],
        out_specs=pl.BlockSpec((groups, rows, 3 * width), lambda i: (i, 0, 0)),
        out_shape=jax.ShapeDtypeStruct((parts, rows, 3 * width), BF),
        compiler_params=params(),
        cost_estimate=cost(2 * rows * model * 3 * ATT, 2 * (3 * ATT * model + rows * 4 * ATT)),
        name="proj_self",
    )(x, qkv_t, qkv_t, qkv_t, cos_rows, sin_rows)


def head_mask(shape, head):
    lane = lax.broadcasted_iota(jnp.int32, shape, 1)
    return lane // HEAD == head


def key_segments(block, block_rows, length, tail):
    stop = (block + 1) * block_rows
    if stop + tail > length:
        return [(0, length)]
    return [(0, stop), (length - tail, length)]


def segment_allowed(segment, q_pos, q_doc, length):
    start, stop = segment
    index = lax.broadcasted_iota(jnp.int32, (1, stop - start), 1) + start
    k_pos = jnp.where(index + SHIFT >= length, index + SHIFT - length, index + SHIFT)
    return (k_pos >= q_doc) & (k_pos <= q_pos)


def query_place(block, block_rows, length):
    index = lax.broadcasted_iota(jnp.int32, (block_rows, 1), 0) + block * block_rows
    return jnp.where(index + SHIFT >= length, index + SHIFT - length, index + SHIFT)


def masked_scores(q_h, k, segs, allowed):
    return [
        jnp.where(ok, mm(q_h, k[a:b], NT), -1e30) for (a, b), ok in zip(segs, allowed)
    ]


def soft(scores):
    top = functools.reduce(jnp.maximum, [jnp.max(s, axis=1, keepdims=True) for s in scores])
    weights = [jnp.exp(s - top) for s in scores]
    total = sum(jnp.sum(e, axis=1, keepdims=True) for e in weights)
    return weights, 1.0 / total


def attn_fwd_kernel(qkv_ref, doc_ref, out_ref, *, block_rows, tail):
    parts, _, tok, width3 = qkv_ref.shape
    width = width3 // 3
    length = parts * tok
    heads = width // HEAD
    per = block_rows // tok
    k = qkv_ref[:, 0, :, width : 2 * width].reshape(length, width)
    v = qkv_ref[:, 0, :, 2 * width :].reshape(length, width)
    for block in range(length // block_rows):
        rows = slice(block * per, (block + 1) * per)
        q = qkv_ref[rows, 0, :, :width].reshape(block_rows, width) * BF(score_scale)
        q_doc = doc_ref[0, block * block_rows : (block + 1) * block_rows, :]
        q_pos = query_place(block, block_rows, length)
        segs = key_segments(block, block_rows, length, tail)
        allowed = [segment_allowed(s, q_pos, q_doc, length) for s in segs]
        mixed = None
        for head in range(heads):
            q_h = jnp.where(head_mask(q.shape, head), q, BF(0)) if heads > 1 else q
            weights, inv = soft(masked_scores(q_h, k, segs, allowed))
            piece = sum(mm(e.astype(BF), v[a:b], NN) for e, (a, b) in zip(weights, segs)) * inv
            mixed = piece if mixed is None else jnp.where(
                head_mask(piece.shape, head), piece, mixed
            )
        out_ref[rows, 0] = mixed.astype(BF).reshape(per, tok, width)


def attn_bwd_kernel(
    qkv_ref, grad_ref, doc_ref, cos_ref, sin_ref, out_ref, dk_ref, dv_ref, *, block_rows, tail
):
    parts, _, tok, width3 = qkv_ref.shape
    width = width3 // 3
    length = parts * tok
    heads = width // HEAD
    per = block_rows // tok
    k = qkv_ref[:, 0, :, width : 2 * width].reshape(length, width)
    v = qkv_ref[:, 0, :, 2 * width :].reshape(length, width)
    dk_ref[...] = jnp.zeros_like(dk_ref)
    dv_ref[...] = jnp.zeros_like(dv_ref)

    def unturn(values, place):
        return values * cos_ref[0, place, :] - half_swap(values) * sin_ref[0, place, :]

    for block in range(length // block_rows):
        rows = slice(block * per, (block + 1) * per)
        place = slice(block * block_rows, (block + 1) * block_rows)
        q = qkv_ref[rows, 0, :, :width].reshape(block_rows, width) * BF(score_scale)
        grad = grad_ref[rows, 0].reshape(block_rows, width)
        q_doc = doc_ref[0, place, :]
        q_pos = query_place(block, block_rows, length)
        segs = key_segments(block, block_rows, length, tail)
        allowed = [segment_allowed(s, q_pos, q_doc, length) for s in segs]
        dq = None
        for head in range(heads):
            q_h = jnp.where(head_mask(q.shape, head), q, BF(0)) if heads > 1 else q
            g_h = jnp.where(head_mask(grad.shape, head), grad, BF(0)) if heads > 1 else grad
            weights, inv = soft(masked_scores(q_h, k, segs, allowed))
            probs = [e * inv for e in weights]
            gp = [mm(g_h, v[a:b], NT) for a, b in segs]
            total = sum(jnp.sum(p * g, axis=1, keepdims=True) for p, g in zip(probs, gp))
            piece = None
            for (a, b), p, g in zip(segs, probs, gp):
                ds = (p * (g - total)).astype(BF)
                dv_ref[a:b, :] += mm(p.astype(BF), g_h, TN)
                dk_ref[a:b, :] += mm(ds, q_h, TN)
                part = mm(ds, k[a:b], NN)
                piece = part if piece is None else piece + part
            dq = piece if dq is None else jnp.where(head_mask(piece.shape, head), piece, dq)
        dq = unturn(dq * score_scale, place)
        out_ref[rows, 0, :, :width] = dq.astype(BF).reshape(per, tok, width)
    for block in range(length // block_rows):
        rows = slice(block * per, (block + 1) * per)
        place = slice(block * block_rows, (block + 1) * block_rows)
        dk = unturn(dk_ref[place, :], place)
        out_ref[rows, 0, :, width : 2 * width] = dk.astype(BF).reshape(per, tok, width)
        out_ref[rows, 0, :, 2 * width :] = (
            dv_ref[place, :].astype(BF).reshape(per, tok, width)
        )


def self_blocks(parts, tok):
    return max(tok, min(256, parts * tok)), min(128, tok)


def attend_self(qkv, doc_col):
    parts, seqs, tok, width3 = qkv.shape
    width = width3 // 3
    length = parts * tok
    block_rows, tail = self_blocks(parts, tok)
    pairs = seqs * (width // HEAD) * length * length
    return pl.pallas_call(
        functools.partial(attn_fwd_kernel, block_rows=block_rows, tail=tail),
        grid=(seqs,),
        in_specs=[
            pl.BlockSpec((parts, 1, tok, width3), lambda i: (0, i, 0, 0)),
            pl.BlockSpec((1, length, 1), lambda i: (i, 0, 0)),
        ],
        out_specs=pl.BlockSpec((parts, 1, tok, width), lambda i: (0, i, 0, 0)),
        out_shape=jax.ShapeDtypeStruct((parts, seqs, tok, width), BF),
        compiler_params=params(),
        cost_estimate=cost(pairs * 512, qkv.size * 3, pairs),
        name="attn_self_fwd",
    )(qkv, doc_col)


def attend_self_back(qkv, grad, doc_col, cos_all, sin_all):
    parts, seqs, tok, width3 = qkv.shape
    width = width3 // 3
    length = parts * tok
    block_rows, tail = self_blocks(parts, tok)
    pairs = seqs * (width // HEAD) * length * length
    rows_spec = pl.BlockSpec((1, length, width), lambda i: (i, 0, 0))
    return pl.pallas_call(
        functools.partial(attn_bwd_kernel, block_rows=block_rows, tail=tail),
        grid=(seqs,),
        in_specs=[
            pl.BlockSpec((parts, 1, tok, width3), lambda i: (0, i, 0, 0)),
            pl.BlockSpec((parts, 1, tok, width), lambda i: (0, i, 0, 0)),
            pl.BlockSpec((1, length, 1), lambda i: (i, 0, 0)),
            rows_spec,
            rows_spec,
        ],
        out_specs=pl.BlockSpec((parts, 1, tok, width3), lambda i: (0, i, 0, 0)),
        out_shape=jax.ShapeDtypeStruct(qkv.shape, BF),
        scratch_shapes=[pltpu.VMEM((length, width), F32), pltpu.VMEM((length, width), F32)],
        compiler_params=params(),
        cost_estimate=cost(pairs * 1280, qkv.size * 6, pairs),
        name="attn_self_bwd",
    )(qkv, grad, doc_col, cos_all, sin_all)


def cross_fwd_kernel(q_ref, k_ref, v_ref, valid_ref, out_ref):
    for pair in range(ATT // 128):
        lanes = slice(pair * 128, (pair + 1) * 128)
        q = q_ref[:, lanes] * BF(score_scale)
        k = k_ref[:, lanes]
        v = v_ref[:, lanes]
        mixed = None
        for head in range(2):
            q_h = jnp.where(head_mask(q.shape, head), q, BF(0))
            (weights,), inv = soft([mm(q_h, k, NT)])
            piece = mm((weights * inv).astype(BF), v, NN)
            mixed = piece if mixed is None else jnp.where(
                head_mask(piece.shape, head), piece, mixed
            )
        out_ref[:, lanes] = (mixed * valid_ref[...]).astype(BF)


def cross_bwd_kernel(q_ref, k_ref, v_ref, valid_ref, grad_ref, dq_ref, dkv_ref):
    for pair in range(ATT // 128):
        lanes = slice(pair * 128, (pair + 1) * 128)
        q = q_ref[:, lanes] * BF(score_scale)
        k = k_ref[:, lanes]
        v = v_ref[:, lanes]
        grad = (grad_ref[:, lanes].astype(F32) * valid_ref[...]).astype(BF)
        dq = dk = dv = None
        for head in range(2):
            q_h = jnp.where(head_mask(q.shape, head), q, BF(0))
            g_h = jnp.where(head_mask(grad.shape, head), grad, BF(0))
            (weights,), inv = soft([mm(q_h, k, NT)])
            probs = weights * inv
            gp = mm(g_h, v, NT)
            total = jnp.sum(probs * gp, axis=1, keepdims=True)
            ds = (probs * (gp - total)).astype(BF)
            part_v = mm(probs.astype(BF), g_h, TN)
            part_k = mm(ds, q_h, TN)
            part_q = mm(ds, k, NN)
            dv = part_v if dv is None else dv + part_v
            dk = part_k if dk is None else dk + part_k
            dq = part_q if dq is None else jnp.where(head_mask(part_q.shape, head), part_q, dq)
        dq_ref[:, lanes] = (dq * score_scale).astype(BF)
        dkv_ref[:, lanes] = dk.astype(BF)
        dkv_ref[:, ATT + pair * 128 : ATT + (pair + 1) * 128] = dv.astype(BF)


def cross_specs(rows, groups, retrieved):
    return [
        pl.BlockSpec((SPAN, ATT), lambda i: (i, 0)),
        pl.BlockSpec((retrieved, ATT), lambda i: (i, 0)),
        pl.BlockSpec((retrieved, ATT), lambda i: (i, 1)),
        pl.BlockSpec((SPAN, 1), lambda i: (i, 0)),
    ]


def attend_cross(query, kv, valid_col):
    rows = query.shape[0]
    groups = rows // SPAN
    retrieved = kv.shape[0] // groups
    return pl.pallas_call(
        cross_fwd_kernel,
        grid=(groups,),
        in_specs=cross_specs(rows, groups, retrieved),
        out_specs=pl.BlockSpec((SPAN, ATT), lambda i: (i, 0)),
        out_shape=jax.ShapeDtypeStruct(query.shape, BF),
        compiler_params=params(),
        cost_estimate=cost(rows * retrieved * ATT * 8, kv.size * 2 + query.size * 4),
        name="attn_cross_fwd",
    )(query, kv, kv, valid_col)


def attend_cross_back(query, kv, valid_col, grad):
    rows = query.shape[0]
    groups = rows // SPAN
    retrieved = kv.shape[0] // groups
    return pl.pallas_call(
        cross_bwd_kernel,
        grid=(groups,),
        in_specs=cross_specs(rows, groups, retrieved)
        + [pl.BlockSpec((SPAN, ATT), lambda i: (i, 0))],
        out_specs=[
            pl.BlockSpec((SPAN, ATT), lambda i: (i, 0)),
            pl.BlockSpec((retrieved, 2 * ATT), lambda i: (i, 0)),
        ],
        out_shape=[
            jax.ShapeDtypeStruct(query.shape, BF),
            jax.ShapeDtypeStruct(kv.shape, BF),
        ],
        compiler_params=params(),
        cost_estimate=cost(rows * retrieved * ATT * 20, kv.size * 4 + query.size * 6),
        name="attn_cross_bwd",
    )(query, kv, kv, valid_col, grad)


def ff_kernel(x_ref, cot_ref, win_ref, wdown_ref, late_ref, out_ref, gx_ref, gw_ref, acc_ref):
    step = pl.program_id(0)
    last = pl.num_programs(0) - 1
    model = x_ref.shape[1]
    x = x_ref[...]
    cot = cot_ref[...]
    u = mm(x, win_ref[...], NT)
    tangent = jnp.tanh(gelu_coef * (u + 0.044715 * u * u * u))
    act = (0.5 * u * (1.0 + tangent)).astype(BF)
    slope = 0.5 * (1.0 + tangent) + 0.5 * u * (1.0 - tangent * tangent) * gelu_coef * (
        1.0 + 3.0 * 0.044715 * u * u
    )
    gp = (mm(cot, wdown_ref[...], NT) * slope).astype(BF)
    gw_ref[:, :model] = mm(gp, x, TN).astype(BF)
    gw_ref[:, model:] = mm(act, cot, TN).astype(BF)
    out_part = mm(act, wdown_ref[...], NN)
    gx_part = mm(gp, win_ref[...], NN)

    @pl.when(step == 0)
    def _():
        acc_ref[...] = late_ref[...] + out_part
        gx_ref[...] = gx_part

    @pl.when(step > 0)
    def _():
        acc_ref[...] += out_part
        gx_ref[...] += gx_part

    @pl.when(step == last)
    def _():
        out_ref[...] = acc_ref[...].astype(BF)


def feed_forward(x, cot, ff_pair, late):
    rows, model = x.shape
    hidden = ff_pair.shape[0]
    block = hidden // 4
    full = lambda i: (0, 0)
    return pl.pallas_call(
        ff_kernel,
        grid=(hidden // block,),
        in_specs=[
            pl.BlockSpec((rows, model), full),
            pl.BlockSpec((rows, model), full),
            pl.BlockSpec((block, model), lambda i: (i, 0)),
            pl.BlockSpec((block, model), lambda i: (i, 1)),
            pl.BlockSpec((rows, model), full),
        ],
        out_specs=[
            pl.BlockSpec((rows, model), full),
            pl.BlockSpec((rows, model), full),
            pl.BlockSpec((block, 2 * model), lambda i: (i, 0)),
        ],
        out_shape=[
            jax.ShapeDtypeStruct((rows, model), BF),
            jax.ShapeDtypeStruct((rows, model), F32),
            jax.ShapeDtypeStruct((hidden, 2 * model), BF),
        ],
        scratch_shapes=[pltpu.VMEM((rows, model), F32)],
        compiler_params=params(),
        cost_estimate=cost(12 * rows * model * hidden, 8 * hidden * model, rows * hidden),
        name="feed_forward",
    )(x, cot, ff_pair, ff_pair, late)


def normalize(values):
    inv_rms = lax.rsqrt(jnp.mean(values * values, axis=-1, keepdims=True) + norm_eps)
    return values * inv_rms, inv_rms


def norm_back(grad_in, normed, inv_rms, gain):
    grad_normed = grad_in * gain
    grad_values = inv_rms * (
        grad_normed - normed * jnp.mean(grad_normed * normed, axis=-1, keepdims=True)
    )
    return grad_values, jnp.sum(grad_in * normed, axis=0)


def shift_in(values):
    count = lax.axis_size("seq")
    later = lax.ppermute(values[:, :SHIFT], "seq", [(i, (i - 1) % count) for i in range(count)])
    return jnp.concatenate([values[:, SHIFT:], later], axis=1)


def shift_out(values):
    count = lax.axis_size("seq")
    keep = values.shape[1] - SHIFT
    earlier = lax.ppermute(values[:, keep:], "seq", [(i, (i + 1) % count) for i in range(count)])
    return jnp.concatenate([earlier, values[:, :keep]], axis=1)


def total_over(values, axis):
    count = lax.axis_size(axis)
    if count & (count - 1):
        return lax.psum(values, axis)
    step = 1
    while step < count:
        values = values + lax.ppermute(values, axis, [(i, i ^ step) for i in range(count)])
        step *= 2
    return values


def on_device(tokens, doc_start, neighbours, qkv_w, out_w, ff_in, ff_out, gains, cotangent):
    parts = lax.axis_size("seq")
    seqs, tok, model = tokens.shape
    rows = seqs * tok
    length = parts * tok
    width = ATT // parts
    here = lax.axis_index("seq")

    qkv_t = lax.all_gather(qkv_w.T, BOTH, axis=0, tiled=True)
    out_t = lax.all_gather(out_w.T, BOTH, axis=0, tiled=True)
    ff_pair = lax.all_gather(
        jnp.concatenate([ff_in.T, ff_out], axis=1), BOTH, axis=0, tiled=True
    )

    doc_all = lax.all_gather(doc_start, "seq", axis=1, tiled=True)
    doc_all = jnp.roll(doc_all, -SHIFT, axis=1)
    place_all = (jnp.arange(length, dtype=jnp.int32) + SHIFT) % length
    frequency = jnp.exp(
        (jnp.arange(width) % (HEAD // 2)).astype(F32) * (-math.log(10000.0) / (HEAD // 2))
    )
    sign = jnp.where(jnp.arange(width) % HEAD < HEAD // 2, -1.0, 1.0).astype(F32)
    angles = (place_all[None] - doc_all).astype(F32)[..., None] * frequency
    cos_all = jnp.cos(angles)
    sin_all = jnp.sin(angles) * sign
    local = lambda table: lax.dynamic_slice_in_dim(table, here * tok, tok, axis=1)
    cos_rows = local(cos_all).reshape(rows, width)
    sin_rows = local(sin_all).reshape(rows, width)
    doc_rows = local(doc_all)
    place = lax.dynamic_slice_in_dim(place_all, here * tok, tok, axis=0)
    doc_col = doc_all[..., None]
    span_of = (place + 1) // SPAN - 1
    valid_col = (
        ((span_of[None] >= 0) & (doc_rows <= span_of[None] * SPAN + SPAN - 1))
        .astype(F32)
        .reshape(rows, 1)
    )

    resid_in = shift_in(tokens).reshape(rows, model).astype(F32)
    cot = shift_in(cotangent).reshape(rows, model)
    nb = neighbours.reshape(-1, model)

    norm_one, inv_one = normalize(resid_in)
    input_one = (norm_one * gains[0]).astype(BF)
    qkv_mine = project_self(input_one, qkv_t, cos_rows, sin_rows, parts)
    qkv_heads = lax.all_to_all(qkv_mine, "seq", 0, 0).reshape(parts, seqs, tok, 3 * width)
    kv = mm(nb, qkv_t[4 * ATT :], NT).astype(BF)
    mixed = attend_self(qkv_heads, doc_col).reshape(parts, rows, width)
    attn_self = lax.all_to_all(mixed, "seq", 0, 0).transpose(1, 0, 2).reshape(rows, ATT)
    resid_mid = resid_in + mm(attn_self, out_t[:model], NT)
    norm_two, inv_two = normalize(resid_mid)
    input_two = (norm_two * gains[1]).astype(BF)
    query_cross = mm(input_two, qkv_t[3 * ATT : 4 * ATT], NT).astype(BF)
    attn_cross = attend_cross(query_cross, kv, valid_col)
    resid_late = resid_mid + mm(attn_cross, out_t[model:], NT)
    norm_three, inv_three = normalize(resid_late)
    input_three = (norm_three * gains[2]).astype(BF)

    output, grad_three, grad_ff = feed_forward(input_three, cot, ff_pair, resid_late)
    shard_ff = lax.psum_scatter(grad_ff, BOTH, scatter_dimension=0, tiled=True)

    back_three, gain_three = norm_back(grad_three, norm_three, inv_three, gains[2])
    grad_late = cot.astype(F32) + back_three
    grad_two = grad_late.astype(BF)
    grad_out_cross = mm(grad_two, attn_cross, TN).astype(BF)
    grad_cross_out = mm(grad_two, out_t[model:], NN).astype(BF)
    grad_query, grad_kv = attend_cross_back(query_cross, kv, valid_col, grad_cross_out)
    grad_neighbours = mm(grad_kv, qkv_t[4 * ATT :], NN)
    grad_w_kv = mm(grad_kv, nb, TN).astype(BF)
    grad_w_q = mm(grad_query, input_two, TN).astype(BF)
    back_two, gain_two = norm_back(
        mm(grad_query, qkv_t[3 * ATT : 4 * ATT], NN), norm_two, inv_two, gains[1]
    )
    grad_mid = grad_late + back_two
    grad_one = grad_mid.astype(BF)
    grad_out_self = mm(grad_one, attn_self, TN).astype(BF)
    grad_attn = mm(grad_one, out_t[:model], NN).astype(BF)
    grad_attn = grad_attn.reshape(rows, parts, width).transpose(1, 0, 2)
    grad_heads = lax.all_to_all(grad_attn, "seq", 0, 0).reshape(parts, seqs, tok, width)
    shard_out = lax.psum_scatter(
        jnp.concatenate([grad_out_self, grad_out_cross], axis=0),
        BOTH,
        scatter_dimension=0,
        tiled=True,
    )
    grad_qkv_heads = attend_self_back(qkv_heads, grad_heads, doc_col, cos_all, sin_all)
    grad_lin = lax.all_to_all(grad_qkv_heads.reshape(parts, rows, 3 * width), "seq", 0, 0)
    grad_lin = grad_lin.reshape(parts, rows, 3, width).transpose(1, 2, 0, 3).reshape(rows, 3 * ATT)
    grad_w_self = mm(grad_lin, input_one, TN).astype(BF)
    shard_qkv = lax.psum_scatter(
        jnp.concatenate([grad_w_self, grad_w_q, grad_w_kv], axis=0),
        BOTH,
        scatter_dimension=0,
        tiled=True,
    )
    back_one, gain_one = norm_back(mm(grad_lin, qkv_t[: 3 * ATT], NN), norm_one, inv_one, gains[0])
    grad_tokens = shift_out((grad_mid + back_one).reshape(seqs, tok, model))
    grad_gains = total_over(
        total_over(jnp.stack([gain_one, gain_two, gain_three]), "seq"), "batch"
    )

    shard_ff = shard_ff.astype(F32)
    return (
        shift_out(output.reshape(seqs, tok, model)),
        grad_tokens,
        grad_neighbours.reshape(neighbours.shape),
        shard_qkv.astype(F32).T,
        shard_out.astype(F32).T,
        shard_ff[:, :model].T,
        shard_ff[:, model:],
        grad_gains,
    )


def solution(mesh):
    rows = P("batch", "seq", None)
    by_column = P(None, BOTH)
    return jax.shard_map(
        on_device,
        mesh=mesh,
        in_specs=(
            rows,
            P("batch", "seq"),
            P("batch", "seq", None, None),
            by_column,
            by_column,
            by_column,
            P(BOTH, None),
            P(),
            rows,
        ),
        out_specs=(
            rows,
            rows,
            P("batch", "seq", None, None),
            by_column,
            by_column,
            by_column,
            P(BOTH, None),
            P(),
        ),
        check_vma=False,
    )
```

time: 3020 us -> 939 us (0.31)
  waiting for transfers between devices: 2050 us -> 469 us
  matrix products: 436 us -> 77.9 us
  local copies, waits for them, and re-layouts: 334 us -> 28.7 us
  Pallas kernels: 0 us -> 189 us
  other arithmetic: 103 us -> 58.1 us
  starting transfers between devices: 18.6 us -> 57.2 us
    all_gather x24 -> x3, waiting for transfers between devices: 1080 us -> 34.7 us  [the longest x1 34.7 us: on_device(): qkv_t = lax.all_gather(qkv_w.T, BOTH, axis=0, tiled=True)]
    while x32 -> x0, waiting for transfers between devices: 465 us -> none
    dot_general x58 -> x14, matrix products: 351 us -> 77.9 us  [mm(): return lax.dot_general(left, right, dims, preferred_element_type=F32)]
    unnamed x13 -> x6, waiting for transfers between devices: 232 us -> 1.94 us
    pallas_call x0 -> x6, Pallas kernels: none -> 189 us  [the longest x1 51.4 us: attend_cross_back(): pl.pallas_call(cross_bwd_kernel, grid=(groups,), in_specs=cross_specs(row...]
    all_to_all x0 -> x4, waiting for transfers between devices: none -> 113 us  [the longest x1 58 us: on_device(): lax.all_to_all(grad_qkv_heads.reshape(parts, rows, 3 * width), 'seq', 0, 0)]
    reduce_scatter x3, waiting for transfers between devices: 162 us -> 255 us  [the longest x1 157 us: on_device(): shard_ff = lax.psum_scatter(grad_ff, BOTH, scatter_dimension=0, tiled=True)]
    sub x12 -> x0, matrix products: 85.9 us -> none  [self_probs(): return jax.nn.softmax(scores, axis=-1)]
  transfers between devices with their start and end apart: 42 -> 19, of which waited for: 36 -> 12; matrix products, arithmetic and copies ran while one was open for 18% -> 15% of each run, Pallas kernels for 0% -> 11%
where the time goes in v1:
time: 939 us; the launch traced here: 932 us
  waiting for transfers between devices  469 us (50%)
  Pallas kernels  189 us (20%)
  matrix products  77.9 us (8%)
  other arithmetic  58.1 us (6%)
  starting transfers between devices  57.2 us (6%)
  blocking collectives  36.5 us (4%)
  local copies, waits for them, and re-layouts  28.7 us (3%)
  between operations  15.2 us (2%)
    reduce_scatter x1, waiting for transfers between devices, on_device(): shard_ff = lax.psum_scatter(grad_ff, BOTH, scatter_dimension=0, tiled=True)  157 us
    reduce_scatter x1, waiting for transfers between devices, on_device(): lax.psum_scatter(jnp.concatenate([grad_w_self, grad_w_q, grad_w_kv], axis...  98.2 us
    dot_general x14, matrix products, mm(): return lax.dot_general(left, right, dims, preferred_element_type=F32)  77.9 us
    ppermute x2, waiting for transfers between devices, shift_in(): lax.ppermute(values[:, :SHIFT], 'seq', [(i, (i - 1) % count) for i in ran...  60.1 us
    all_to_all x1, waiting for transfers between devices, on_device(): lax.all_to_all(grad_qkv_heads.reshape(parts, rows, 3 * width), 'seq', 0, 0)  58 us
    pallas_call x1, Pallas kernels, attend_cross_back(): pl.pallas_call(cross_bwd_kernel, grid=(groups,), in_specs=cross_specs(row...  51.4 us
    pallas_call x1, Pallas kernels, attend_cross(): pl.pallas_call(cross_fwd_kernel, grid=(groups,), in_specs=cross_specs(row...  44.4 us
    all_gather x1, blocking collectives, on_device(): doc_all = lax.all_gather(doc_start, 'seq', axis=1, tiled=True)  36.5 us
  transfers between devices with their start and end apart: 19, of which 12 were waited for; matrix products, arithmetic and copies ran while one was open for 15% of the time, Pallas kernels for 11%

profile of v1, /device:TPU:0, one launch (start us, length us, event | category | flops | bytes accessed | tf_op | source)
XLA Modules:
  0.0 931.9 jit_solution(13687579483914244857)
XLA Ops:
  11.4 6.0 collective-permute-start
  17.4 36.5 %all_gather.13 = s32[4,1024]{1,0:T(4,128)S(1)} all-gather(s32[4,128]{1,0:T(4,128)S(1)} %copy-done.29), channel_id=1, replica_groups=mesh['seq'=8,'batch'=4] {'seq'}, dimensions={1}, use_global_device_ids=true | all-gather | bytes 18432 | tf_op jit(solution)/shard_map/all_gather | solution.py:468
  54.6 8.7 fusion.5
  70.1 34.7 %all-gather.4.cloned.1.call-done.wq_ref.wk_ref.wv_ref = bf16[6144,896]{1,0:T(8,128)(2,1)} async-done(((bf16[192,896]{1,0:T(8,128)(2,1)}), bf16[6144,896]{1,0:T(8,128)(2,1)}) %all-gather.4.cloned.1.call-update) | async-done | bytes 11010064 | tf_op jit(solution)/shard_map/all_gather | solution.py:462
  104.8 8.2 proj_self.1
  113.0 4.6 all-to-all-start
  117.7 4.7 collective-permute-start.1
  126.1 60.1 %collective-permute-done.1 = bf16[4,63,896]{2,1,0:T(8,128)(2,1)S(1)} collective-permute-done((bf16[4,63,896]{2,1,0:T(8,128)(2,1)S(1)}, bf16[4,63,896]{2,1,0:T(8,128)(2,1)S(1)}, u32[]{:S(2)}, u32[]{:S(2)}) %collective-permute-start.1) | collective-permute-done | bytes 451616 | tf_op jit(solution)/shard_map/ppermute | solution.py:432
  187.3 8.6 all-to-all-done
  195.9 16.8 %attn_self_fwd.1 = bf16[8,4,128,128]{3,2,1,0:T(8,128)(2,1)} custom-call(bf16[8,4,128,384]{3,2,1,0:T(8,128)(2,1)} %bitcast.5.qkv_ref, s32[4,1024,1]{2,1,0:T(8,128)} %copy.34.doc_ref), custom_call_target="tpu_custom_call" | custom-call | flops 4294967296 | bytes 4718592 | tf_op jit(solution)/shard_map/attn_self_fwd/pallas_call | solution.py:219
  215.0 23.2 %all-to-all-start.1 = ((bf16[8,512,128]{1,2,0:T(8,128)(2,1)}), bf16[8,512,128]{1,2,0:T(8,128)(2,1)S(1)}, u32[]{:S(2)}, u32[]{:S(2)}) async-start(bf16[8,512,128]{1,2,0:T(8,128)(2,1)} %copy.35), calls=%async_computation.1 | async-start | bytes 2097152 | tf_op jit(solution)/shard_map/all_to_all | solution.py:501
  238.3 13.8 %convolution_convert_fusion.k_ref.v_ref = bf16[2048,2048]{1,0:T(8,128)(2,1)} fusion(bf16[2048,896]{1,0:T(8,128)(2,1)} %bitcast.97, bf16[6144,896]{1,0:T(8,128)(2,1)} %all-gather.4.cloned.1.call-done.wq_ref.wk_ref.wv_ref), kind=kOutput, calls=%fused_computation.1 | convolution fusion | flops 7520387072 | bytes 15728640 | tf_op jit(solution)/shard_map/dot_general | solution.py:30
  252.0 25.9 %all-to-all-done.1 = bf16[8,512,128]{1,2,0:T(8,128)(2,1)S(1)} async-done(((bf16[8,512,128]{1,2,0:T(8,128)(2,1)}), bf16[8,512,128]{1,2,0:T(8,128)(2,1)S(1)}, u32[]{:S(2)}, u32[]{:S(2)}) %all-to-all-start.1) | async-done | bytes 1048608 | tf_op jit(solution)/shard_map/all_to_all | solution.py:501
  282.5 3.8 fusion.34.q_ref
  286.3 44.4 %attn_cross_fwd.1 = bf16[512,1024]{1,0:T(8,128)(2,1)} custom-call(bf16[512,1024]{1,0:T(8,128)(2,1)} %fusion.34.q_ref, bf16[2048,2048]{1,0:T(8,128)(2,1)} %convolution_convert_fusion.k_ref.v_ref, bf16[2048,2048]{1,0:T(8,128)(2,1)} %convolution_convert_fusion.k_ref.v_ref, f32[512,1]{1,0:T(8,128)} %copy.36.valid_ref), custom_call_target="tpu_custom_call" | custom-call | flops 1073741824 | bytes 10485760 | tf_op jit(solution)/shard_map/attn_cross_fwd/pallas_call | solution.py:317
  330.7 3.7 multiply_reduce_fusion.4
  336.0 33.4 %feed_forward.1 = (bf16[512,896]{1,0:T(8,128)(2,1)}, f32[512,896]{1,0:T(8,128)}, bf16[3584,1792]{1,0:T(8,128)(2,1)}) custom-call(bf16[512,896]{1,0:T(8,128)(2,1)} %multiply_convert_fusion.x_ref, bf16[512,896]{1,0:T(8,128)(2,1)} %bitcast.81, bf16[3584,1792]{1,0:T(8,128)(2,1)} %all-gather.8.cloned.1.call-done.win_ref.wdown_ref, ...), custom_call_target="tpu_custom_call" | custom-call | flops 19730006016 | bytes 25690112 | tf_op jit(solution)/shard_map/feed_forward/pallas_call | solution.py:390
  377.9 51.4 %attn_cross_bwd.1 = (bf16[512,1024]{1,0:T(8,128)(2,1)}, bf16[2048,2048]{1,0:T(8,128)(2,1)}) custom-call(bf16[512,1024]{1,0:T(8,128)(2,1)} %fusion.34.q_ref, bf16[2048,2048]{1,0:T(8,128)(2,1)} %convolution_convert_fusion.k_ref.v_ref, bf16[2048,2048]{1,0:T(8,128)(2,1)} %convolution_convert_fusion.k_ref.v_ref, f32[512,1]{1,0:T(8,128)} %copy.36.valid_ref, ...), custom_call_target="tpu_custom_call" | custom-call | flops 2684354560 | bytes 19922944 | tf_op jit(solution)/shard_map/attn_cross_bwd/pallas_call | solution.py:333
  437.2 4.2 all-to-all-start.2
  447.4 20.4 %all-to-all-done.2 = bf16[8,512,128]{2,1,0:T(8,128)(2,1)} async-done(((bf16[8,512,128]{2,1,0:T(8,128)(2,1)}), bf16[8,512,128]{2,1,0:T(8,128)(2,1)}, u32[]{:S(2)}, u32[]{:S(2)}) %all-to-all-start.2) | async-done | bytes 1048608 | tf_op jit(solution)/shard_map/all_to_all | solution.py:531
  467.8 35.1 %attn_self_bwd.1 = bf16[8,4,128,384]{3,2,1,0:T(8,128)(2,1)} custom-call(bf16[8,4,128,384]{3,2,1,0:T(8,128)(2,1)} %bitcast.5.qkv_ref, bf16[8,4,128,128]{3,2,1,0:T(8,128)(2,1)} %bitcast.17.grad_ref, s32[4,1024,1]{2,1,0:T(8,128)} %copy.34.doc_ref, f32[4,1024,128]{2,1,0:T(8,128)} %get-tuple-element.34.cos_ref, f32[4,1024,128]{2,1,0:T(8,128)} %copy-done.10), custom_call_target="tpu_custom_call" | custom-call | flops 10737418240 | bytes 9437184 | tf_op jit(solution)/shard_map/attn_self_bwd/pallas_call | solution.py:241
  503.0 4.7 copy.40
  507.6 4.5 all-to-all-start.3
  514.0 4.0 convolution_convert_fusion.5
  517.9 12.9 %convolution_convert_fusion.2 = bf16[2048,896]{1,0:T(8,128)(2,1)} fusion(bf16[2048,2048]{1,0:T(8,128)(2,1)} %get-tuple-element.16, bf16[2048,896]{1,0:T(8,128)(2,1)S(1)} %bitcast.98), kind=kOutput, calls=%fused_computation.6 | convolution fusion | flops 7518027776 | bytes 15728640 | tf_op jit(solution)/shard_map/dot_general | solution.py:30
  530.8 58.0 %all-to-all-done.3 = bf16[8,512,384]{1,2,0:T(8,128)(2,1)} async-done(((bf16[8,512,384]{1,2,0:T(8,128)(2,1)}), bf16[8,512,384]{1,2,0:T(8,128)(2,1)}, u32[]{:S(2)}, u32[]{:S(2)}) %all-to-all-start.3) | async-done | bytes 3145760 | tf_op jit(solution)/shard_map/all_to_all | solution.py:539
  594.8 24.3 %pad_maximum_fusion = bf16[6144,896]{1,0:T(8,128)(2,1)} fusion(bf16[2048,896]{1,0:T(8,128)(2,1)S(1)} %copy-done.8, bf16[1024,896]{1,0:T(8,128)(2,1)S(1)} %copy-done.15, bf16[3072,896]{1,0:T(8,128)(2,1)S(1)} %convolution_convert_fusion.1), kind=kLoop, calls=%fused_computation | loop fusion | flops 33030144 | bytes 22020096 | tf_op jit(solution)/shard_map/concatenate | solution.py:543
  620.5 7.7 fusion.15
  637.8 3.9 collective-permute-start.6
  641.7 14.5 %fusion.2 = f32[2048,896]{1,0:T(8,128)} fusion(bf16[2048,2048]{1,0:T(8,128)(2,1)} %get-tuple-element.16, bf16[6144,896]{1,0:T(8,128)(2,1)} %all-gather.4.cloned.1.call-done.wq_ref.wk_ref.wv_ref), kind=kOutput, calls=%fused_computation.7 | convolution fusion | flops 7516192768 | bytes 19398656 | tf_op jit(solution)/shard_map/dot_general | solution.py:30
  665.3 98.2 %reduce-scatter.4.cloned.1.call-done = bf16[192,896]{1,0:T(8,128)(2,1)} async-done(((bf16[6144,896]{1,0:T(8,128)(2,1)}), bf16[192,896]{1,0:T(8,128)(2,1)}) %reduce-scatter.4.cloned.1.call-update) | async-done | bytes 344080 | tf_op jit(solution)/shard_map/reduce_scatter | solution.py:542
  765.4 156.5 %reduce-scatter.8.cloned.1.call-done = bf16[112,1792]{1,0:T(8,128)(2,1)} async-done(((bf16[3584,1792]{1,0:T(8,128)(2,1)}), bf16[112,1792]{1,0:T(8,128)(2,1)}) %reduce-scatter.8.cloned.1.call-update) | async-done | bytes 401424 | tf_op jit(solution)/shard_map/reduce_scatter | solution.py:512
  (161 shorter events, 79.4 us)
Async XLA Ops:
  7.2 10.2 %copy-start.29 = (s32[4,128]{1,0:T(4,128)S(1)}, s32[4,128]{1,0:T(4,128)}, u32[]{:S(2)}) copy-start(s32[4,128]{1,0:T(4,128)} %param.10) | copy-start | bytes 6148
  7.2 97.6 %all-gather.4.cloned.1.call-start = ((), (), s32[]{:S(2)}) async-start(), calls=%async_computation.7 | async-start | bytes 11354112 | tf_op jit(solution)/shard_map/all_gather | solution.py:462
  7.9 244.1 %all-gather.6.cloned.1.call-start = ((), (), s32[]{:S(2)}) async-start(), calls=%async_computation.8 | async-start | bytes 3784704 | tf_op jit(solution)/shard_map/all_gather | solution.py:463
  8.7 327.1 %all-gather.8.cloned.1.call-start = ((), (), s32[]{:S(2)}) async-start(), calls=%async_computation.9 | async-start | bytes 13246464 | tf_op jit(solution)/shard_map/all_gather | solution.py:464
  11.4 56.0 %collective-permute-start = (bf16[4,63,896]{2,1,0:T(8,128)(2,1)}, bf16[4,63,896]{2,1,0:T(8,128)(2,1)}, u32[]{:S(2)}, u32[]{:S(2)}) collective-permute-start(bf16[4,63,896]{2,1,0:T(8,128)(2,1)} %slice.70), channel_id=1, source_target_pairs={{0,28},{4,0},{8,4},{12,8},{16,12},{20,16},{24,20},{28,24},{1,29},{... | collective-permute-start | bytes 1354760 | tf_op jit(solution)/shard_map/ppermute | solution.py:432
  53.9 9.4 %copy-start.26 = (s32[4,63]{1,0:T(4,128)}, s32[4,63]{1,0:T(4,128)S(1)}, u32[]{:S(2)}) copy-start(s32[4,63]{1,0:T(4,128)S(1)} %slice.90) | copy-start | bytes 3028
  53.9 9.4 %copy-start.25 = (s32[1024]{0:T(1024)}, s32[1024]{0:T(1024)S(1)}, u32[]{:S(2)}) copy-start(s32[1024]{0:T(1024)S(1)} %add_select_fusion) | copy-start | bytes 12292
  63.4 5.5 copy-start.10
  113.0 4.6 copy-start.20
  113.0 83.0 %all-to-all-start = ((bf16[8,512,384]{2,1,0:T(8,128)(2,1)}), bf16[8,512,384]{2,1,0:T(8,128)(2,1)}, u32[]{:S(2)}, u32[]{:S(2)}) async-start(bf16[8,512,384]{2,1,0:T(8,128)(2,1)} %proj_self.1), calls=%async_computation | async-start | bytes 6291456 | tf_op jit(solution)/shard_map/all_to_all | solution.py:498
  117.6 5.6 copy-start.24
  117.6 7.6 copy-start.27
  117.7 68.6 %collective-permute-start.1 = (bf16[4,63,896]{2,1,0:T(8,128)(2,1)S(1)}, bf16[4,63,896]{2,1,0:T(8,128)(2,1)S(1)}, u32[]{:S(2)}, u32[]{:S(2)}) collective-permute-start(bf16[4,63,896]{2,1,0:T(8,128)(2,1)S(1)} %slice.81), channel_id=1, source_target_pairs={{0,28},{4,0},{8,4},{12,8},{16,12},{20,16},{24,20},{28,24},{1,29},{... | collective-permute-start | bytes 1354760 | tf_op jit(solution)/shard_map/ppermute | solution.py:432
  215.0 62.9 %all-to-all-start.1 = ((bf16[8,512,128]{1,2,0:T(8,128)(2,1)}), bf16[8,512,128]{1,2,0:T(8,128)(2,1)S(1)}, u32[]{:S(2)}, u32[]{:S(2)}) async-start(bf16[8,512,128]{1,2,0:T(8,128)(2,1)} %copy.35), calls=%async_computation.1 | async-start | bytes 2097152 | tf_op jit(solution)/shard_map/all_to_all | solution.py:501
  277.9 4.5 copy-start.28
  377.9 51.4 %copy-start.12 = (f32[512,896]{1,0:T(8,128)S(1)}, f32[512,896]{1,0:T(8,128)}, u32[]{:S(2)}) copy-start(f32[512,896]{1,0:T(8,128)} %copy-done.11) | copy-start | bytes 5505028
  434.7 6.8 copy-start.2
  437.2 30.7 %all-to-all-start.2 = ((bf16[8,512,128]{2,1,0:T(8,128)(2,1)}), bf16[8,512,128]{2,1,0:T(8,128)(2,1)}, u32[]{:S(2)}, u32[]{:S(2)}) async-start(bf16[8,512,128]{2,1,0:T(8,128)(2,1)} %bitcast.80), calls=%async_computation.2 | async-start | bytes 2097152 | tf_op jit(solution)/shard_map/all_to_all | solution.py:531
  441.4 216.1 %reduce-scatter.6.cloned.1.call-start = ((), (), s32[]{:S(2)}) async-start(), calls=%async_computation.11 | async-start | bytes 3784704 | tf_op jit(solution)/shard_map/reduce_scatter | solution.py:532
  507.6 81.2 %all-to-all-start.3 = ((bf16[8,512,384]{1,2,0:T(8,128)(2,1)}), bf16[8,512,384]{1,2,0:T(8,128)(2,1)}, u32[]{:S(2)}, u32[]{:S(2)}) async-start(bf16[8,512,384]{1,2,0:T(8,128)(2,1)} %copy.40), calls=%async_computation.3 | async-start | bytes 6291456 | tf_op jit(solution)/shard_map/all_to_all | solution.py:539
  512.1 251.4 %reduce-scatter.4.cloned.1.call-start = ((), (), s32[]{:S(2)}) async-start(), calls=%async_computation.10 | async-start | bytes 11354112 | tf_op jit(solution)/shard_map/reduce_scatter | solution.py:542
  514.0 4.0 copy-start.30
  619.1 302.9 %reduce-scatter.8.cloned.1.call-start = ((), (), s32[]{:S(2)}) async-start(), calls=%async_computation.12 | async-start | bytes 13246464 | tf_op jit(solution)/shard_map/reduce_scatter | solution.py:512
  620.4 15.3 %copy-start.3 = (f32[512,896]{1,0:T(8,128)S(1)}, f32[512,896]{1,0:T(8,128)}, u32[]{:S(2)}) copy-start(f32[512,896]{1,0:T(8,128)} %copy-done.2) | copy-start | bytes 5505028
  620.4 35.9 %collective-permute-start.2 = (bf16[4,63,896]{2,1,0:T(8,128)(2,1)S(1)}, bf16[4,63,896]{2,1,0:T(8,128)(2,1)S(1)}, u32[]{:S(2)}, u32[]{:S(2)}) collective-permute-start(bf16[4,63,896]{2,1,0:T(8,128)(2,1)S(1)} %slice.95), channel_id=1, source_target_pairs={{0,4},{4,8},{8,12},{12,16},{16,20},{20,24},{24,28},{28,0},{1,5},{5... | collective-permute-start | bytes 1354760 | tf_op jit(solution)/shard_map/ppermute | solution.py:439
  628.2 4.9 collective-permute-start.4
  633.2 4.6 collective-permute-start.5
  637.7 24.9 %collective-permute-start.3 = (f32[4,63,896]{2,0,1:T(4,128)}, f32[4,63,896]{2,0,1:T(4,128)}, u32[]{:S(2)}, u32[]{:S(2)}) collective-permute-start(f32[4,63,896]{2,0,1:T(4,128)} %copy.44), channel_id=1, source_target_pairs={{0,4},{4,8},{8,12},{12,16},{16,20},{20,24},{24,28},{28,0},{1,5},{5... | collective-permute-start | bytes 2709512 | tf_op jit(solution)/shard_map/ppermute | solution.py:439
  637.8 18.4 %copy-start.22 = (bf16[512,896]{1,0:T(8,128)(2,1)S(1)}, bf16[512,896]{1,0:T(8,128)(2,1)}, u32[]{:S(2)}) copy-start(bf16[512,896]{1,0:T(8,128)(2,1)} %get-tuple-element.13) | copy-start | bytes 2752516
  637.8 18.5 %collective-permute-start.6 = (f32[3,896]{1,0:T(4,128)S(1)}, f32[3,896]{1,0:T(4,128)S(1)}, u32[]{:S(2)}, u32[]{:S(2)}) collective-permute-start(f32[3,896]{1,0:T(4,128)S(1)} %fusion.78), channel_id=1, source_target_pairs={{0,16},{4,20},{8,24},{12,28},{16,0},{20,4},{24,8},{28,12},{1,17},{... | collective-permute-start | bytes 32264 | tf_op jit(solution)/shard_map/ppermute | solution.py:449
  656.3 1.2 collective-permute-start.7
  657.5 3.7 collective-permute-start.8
  (20 other events, 52.0 us)
Sparse Core Ops, SparseCore 0:
  10.9 93.8 all-gather.3
  107.7 105.4 all-gather.5
  216.6 112.3 all-gather.7
  447.6 148.9 reduce-scatter.5
  619.2 144.3 reduce-scatter.3
  765.8 156.0 reduce-scatter.7

commit v2 on v1

--- a/solution.py
+++ b/solution.py
@@ -440,15 +440,117 @@
     return jnp.concatenate([earlier, values[:, :keep]], axis=1)
 
 
+def paired(values, axis, stride):
+    count = lax.axis_size(axis)
+    return lax.ppermute(values, axis, [(i, i ^ stride) for i in range(count)])
+
+
+def bit_of(axis, stride):
+    return (lax.axis_index(axis) // stride) % 2
+
+
+def bits_of(axis):
+    count = lax.axis_size(axis)
+    return [(axis, 1 << k) for k in range(count.bit_length() - 1)]
+
+
+def index_bits():
+    bits = bits_of("seq")[:-1][::-1] + bits_of("batch")[::-1]
+    return {bit: dim for dim, bit in enumerate(bits)}
+
+
+def top_bit():
+    return bits_of("seq")[-1]
+
+
+def stage_orders():
+    core, *across = bits_of("batch")
+    low, *along = bits_of("seq")[:-1]
+    return core, (across + [low], [low] + across), along
+
+
 def total_over(values, axis):
-    count = lax.axis_size(axis)
-    if count & (count - 1):
-        return lax.psum(values, axis)
-    step = 1
-    while step < count:
-        values = values + lax.ppermute(values, axis, [(i, i ^ step) for i in range(count)])
-        step *= 2
+    for bit in bits_of(axis):
+        values = values + paired(values, *bit)
     return values
+
+
+def grown(values, bit, dim):
+    other = paired(values, *bit)
+    both = jnp.stack([other, other], axis=dim)
+    return lax.dynamic_update_index_in_dim(both, values, bit_of(*bit), dim)
+
+
+def pick(values, index, dim):
+    return lax.dynamic_index_in_dim(values, index, dim, keepdims=False)
+
+
+def halved(values, bit, dim):
+    mine = bit_of(*bit)
+    other = paired(pick(values, 1 - mine, dim), *bit)
+    return (pick(values, mine, dim).astype(F32) + other.astype(F32)).astype(BF)
+
+
+def gather_half(piece, split):
+    dims = index_bits()
+    core, orders, along = stage_orders()
+    held = []
+
+    def grow(values, bit):
+        dim = sum(dims[b] < dims[bit] for b in held)
+        held.append(bit)
+        return grown(values, bit, dim)
+
+    for bit in along[::-1]:
+        piece = grow(piece, bit)
+    base = list(held)
+    colors = []
+    for part, order in zip(jnp.split(piece, 2, axis=piece.ndim - 2 + split), orders):
+        held[:] = base
+        for bit in order[::-1]:
+            part = grow(part, bit)
+        colors.append(part)
+    last = len(dims) - 1
+    shape = list(colors[0].shape)
+    shape.insert(last, 2)
+    shape.insert(last + 1 + split, 2)
+    whole = jnp.zeros(shape, colors[0].dtype)
+    mine = bit_of(*core)
+    for k, part in enumerate(colors):
+        for slot, values in ((mine, part), (1 - mine, paired(part, *core))):
+            block = jnp.expand_dims(jnp.expand_dims(values, last), last + 1 + split)
+            start = [0] * len(shape)
+            start[last] = slot
+            start[last + 1 + split] = k
+            whole = lax.dynamic_update_slice(whole, block, start)
+    columns = shape[-1] * (2 if split else 1)
+    return whole.reshape(-1, columns)
+
+
+def scatter_half(grads, rows, split, owner):
+    dims = index_bits()
+    core, orders, along = stage_orders()
+    columns = grads.shape[1]
+    grid = grads.reshape([2] * len(dims) + [rows, columns])
+    results = []
+    for k, order in enumerate(orders):
+        part = lax.slice_in_dim(
+            grid,
+            k * grid.shape[len(dims) + split] // 2,
+            (k + 1) * grid.shape[len(dims) + split] // 2,
+            axis=len(dims) + split,
+        )
+        left = dict(dims)
+        for bit in [core] + order + along:
+            dim = sum(left[b] < left[bit] for b in left)
+            part = halved(part, bit, dim)
+            del left[bit]
+        axis, stride = top_bit()
+        count = lax.axis_size(axis)
+        senders = [i for i in range(count) if (i // stride) % 2 != owner]
+        other = lax.ppermute(part, axis, [(i, i ^ stride) for i in senders])
+        results.append(part.astype(F32) + other.astype(F32))
+    return jnp.concatenate(results, axis=split)
 
 
 def on_device(tokens, doc_start, neighbours, qkv_w, out_w, ff_in, ff_out, gains, cotangent):
@@ -459,14 +561,21 @@
     width = ATT // parts
     here = lax.axis_index("seq")
 
-    qkv_t = lax.all_gather(qkv_w.T, BOTH, axis=0, tiled=True)
+    upper = bit_of(*top_bit()) == 1
+    qkv_own = qkv_w.T
+    qkv_other = paired(qkv_own, *top_bit())
+    w_self = gather_half(jnp.where(upper, qkv_other, qkv_own), 0)
+    w_cross = gather_half(jnp.where(upper, qkv_own, qkv_other), 0)
+    w_q, w_kv = w_cross[:ATT], w_cross[ATT:]
     out_t = lax.all_gather(out_w.T, BOTH, axis=0, tiled=True)
     ff_pair = lax.all_gather(
         jnp.concatenate([ff_in.T, ff_out], axis=1), BOTH, axis=0, tiled=True
     )
 
-    doc_all = lax.all_gather(doc_start, "seq", axis=1, tiled=True)
-    doc_all = jnp.roll(doc_all, -SHIFT, axis=1)
+    doc_all = doc_start[None]
+    for bit in bits_of("seq"):
+        doc_all = grown(doc_all, bit, 0).reshape(-1, seqs, tok)
+    doc_all = jnp.roll(doc_all.transpose(1, 0, 2).reshape(seqs, length), -SHIFT, axis=1)
     place_all = (jnp.arange(length, dtype=jnp.int32) + SHIFT) % length
     frequency = jnp.exp(
         (jnp.arange(width) % (HEAD // 2)).astype(F32) * (-math.log(10000.0) / (HEAD // 2))
@@ -494,15 +603,15 @@
 
     norm_one, inv_one = normalize(resid_in)
     input_one = (norm_one * gains[0]).astype(BF)
-    qkv_mine = project_self(input_one, qkv_t, cos_rows, sin_rows, parts)
+    qkv_mine = project_self(input_one, w_self, cos_rows, sin_rows, parts)
     qkv_heads = lax.all_to_all(qkv_mine, "seq", 0, 0).reshape(parts, seqs, tok, 3 * width)
-    kv = mm(nb, qkv_t[4 * ATT :], NT).astype(BF)
+    kv = mm(nb, w_kv, NT).astype(BF)
     mixed = attend_self(qkv_heads, doc_col).reshape(parts, rows, width)
     attn_self = lax.all_to_all(mixed, "seq", 0, 0).transpose(1, 0, 2).reshape(rows, ATT)
     resid_mid = resid_in + mm(attn_self, out_t[:model], NT)
     norm_two, inv_two = normalize(resid_mid)
     input_two = (norm_two * gains[1]).astype(BF)
-    query_cross = mm(input_two, qkv_t[3 * ATT : 4 * ATT], NT).astype(BF)
+    query_cross = mm(input_two, w_q, NT).astype(BF)
     attn_cross = attend_cross(query_cross, kv, valid_col)
     resid_late = resid_mid + mm(attn_cross, out_t[model:], NT)
     norm_three, inv_three = normalize(resid_late)
@@ -517,11 +626,11 @@
     grad_out_cross = mm(grad_two, attn_cross, TN).astype(BF)
     grad_cross_out = mm(grad_two, out_t[model:], NN).astype(BF)
     grad_query, grad_kv = attend_cross_back(query_cross, kv, valid_col, grad_cross_out)
-    grad_neighbours = mm(grad_kv, qkv_t[4 * ATT :], NN)
+    grad_neighbours = mm(grad_kv, w_kv, NN)
     grad_w_kv = mm(grad_kv, nb, TN).astype(BF)
     grad_w_q = mm(grad_query, input_two, TN).astype(BF)
     back_two, gain_two = norm_back(
-        mm(grad_query, qkv_t[3 * ATT : 4 * ATT], NN), norm_two, inv_two, gains[1]
+        mm(grad_query, w_q, NN), norm_two, inv_two, gains[1]
     )
     grad_mid = grad_late + back_two
     grad_one = grad_mid.astype(BF)
@@ -529,23 +638,23 @@
     grad_attn = mm(grad_one, out_t[:model], NN).astype(BF)
     grad_attn = grad_attn.reshape(rows, parts, width).transpose(1, 0, 2)
     grad_heads = lax.all_to_all(grad_attn, "seq", 0, 0).reshape(parts, seqs, tok, width)
-    shard_out = lax.psum_scatter(
-        jnp.concatenate([grad_out_self, grad_out_cross], axis=0),
-        BOTH,
-        scatter_dimension=0,
-        tiled=True,
+    out_rows = 2 * model // (parts * lax.axis_size("batch"))
+    qkv_rows = 6 * ATT // (parts * lax.axis_size("batch"))
+    shard_out = jnp.where(
+        upper,
+        scatter_half(grad_out_cross, out_rows, 1, 1),
+        scatter_half(grad_out_self, out_rows, 1, 0),
     )
     grad_qkv_heads = attend_self_back(qkv_heads, grad_heads, doc_col, cos_all, sin_all)
     grad_lin = lax.all_to_all(grad_qkv_heads.reshape(parts, rows, 3 * width), "seq", 0, 0)
     grad_lin = grad_lin.reshape(parts, rows, 3, width).transpose(1, 2, 0, 3).reshape(rows, 3 * ATT)
     grad_w_self = mm(grad_lin, input_one, TN).astype(BF)
-    shard_qkv = lax.psum_scatter(
-        jnp.concatenate([grad_w_self, grad_w_q, grad_w_kv], axis=0),
-        BOTH,
-        scatter_dimension=0,
-        tiled=True,
-    )
-    back_one, gain_one = norm_back(mm(grad_lin, qkv_t[: 3 * ATT], NN), norm_one, inv_one, gains[0])
+    shard_qkv = jnp.where(
+        upper,
+        scatter_half(jnp.concatenate([grad_w_q, grad_w_kv], axis=0), qkv_rows, 0, 1),
+        scatter_half(grad_w_self, qkv_rows, 0, 0),
+    )
+    back_one, gain_one = norm_back(mm(grad_lin, w_self, NN), norm_one, inv_one, gains[0])
     grad_tokens = shift_out((grad_mid + back_one).reshape(seqs, tok, model))
     grad_gains = total_over(
         total_over(jnp.stack([gain_one, gain_two, gain_three]), "seq"), "batch"
@@ -556,8 +665,8 @@
         shift_out(output.reshape(seqs, tok, model)),
         grad_tokens,
         grad_neighbours.reshape(neighbours.shape),
-        shard_qkv.astype(F32).T,
-        shard_out.astype(F32).T,
+        shard_qkv.T,
+        shard_out.T,
         shard_ff[:, :model].T,
         shard_ff[:, model:],
         grad_gains,

time: 939 us -> 858 us (0.914)
  waiting for transfers between devices: 469 us -> 341 us
  starting transfers between devices: 57.2 us -> 117 us
  blocking collectives: 36.5 us -> 0 us
  local copies, waits for them, and re-layouts: 28.7 us -> 60.8 us
    ppermute x5 -> x63, waiting for transfers between devices: 3.78 us -> 313 us  [the longest x55 289 us: paired(): return lax.ppermute(values, axis, [(i, i ^ stride) for i in range(count)])]
    reduce_scatter x1, waiting for transfers between devices: 157 us -> 0.01 us  [on_device(): shard_ff = lax.psum_scatter(grad_ff, BOTH, scatter_dimension=0, tiled=True)]
    reduce_scatter x2 -> x0, waiting for transfers between devices: 98.3 us -> none  [the longest x1 98.2 us: on_device(): lax.psum_scatter(jnp.concatenate([grad_w_self, grad_w_q, grad_w_kv], axis...]
    ppermute x5 -> x63, starting transfers between devices: 9.74 us -> 86.7 us  [the longest x55 69.5 us: paired(): return lax.ppermute(values, axis, [(i, i ^ stride) for i in range(count)])]
    ppermute x2, waiting for transfers between devices: 60.1 us -> 0.01 us  [shift_in(): lax.ppermute(values[:, :SHIFT], 'seq', [(i, (i - 1) % count) for i in ran...]
    all_to_all x1, waiting for transfers between devices: 58 us -> 0.01 us  [on_device(): lax.all_to_all(grad_qkv_heads.reshape(parts, rows, 3 * width), 'seq', 0, 0)]
    all_gather x1 -> x0, blocking collectives: 36.5 us -> none  [on_device(): doc_all = lax.all_gather(doc_start, 'seq', axis=1, tiled=True)]
    all_gather x1 -> x0, waiting for transfers between devices: 34.7 us -> none  [on_device(): qkv_t = lax.all_gather(qkv_w.T, BOTH, axis=0, tiled=True)]
  transfers between devices with their start and end apart: 19 -> 74, of which waited for: 12 -> 30; matrix products, arithmetic and copies ran while one was open for 15% -> 19% of each run, Pallas kernels for 11% -> 12%
where the time goes in v2:
time: 858 us; the launch traced here: 847 us
  waiting for transfers between devices  341 us (40%)
  Pallas kernels  190 us (22%)
  starting transfers between devices  117 us (14%)
  matrix products  72 us (8%)
  local copies, waits for them, and re-layouts  60.8 us (7%)
  other arithmetic  50.4 us (6%)
  between operations  15.9 us (2%)
    ppermute x55, waiting for transfers between devices, paired(): return lax.ppermute(values, axis, [(i, i ^ stride) for i in range(count)])  289 us
    dot_general x14, matrix products, mm(): return lax.dot_general(left, right, dims, preferred_element_type=F32)  72 us
    ppermute x55, starting transfers between devices, paired(): return lax.ppermute(values, axis, [(i, i ^ stride) for i in range(count)])  69.5 us
    pallas_call x1, Pallas kernels, attend_cross_back(): pl.pallas_call(cross_bwd_kernel, grid=(groups,), in_specs=cross_specs(row...  51.6 us
    pallas_call x1, Pallas kernels, attend_cross(): pl.pallas_call(cross_fwd_kernel, grid=(groups,), in_specs=cross_specs(row...  44 us
    pallas_call x1, Pallas kernels, attend_self_back(): pl.pallas_call(functools.partial(attn_bwd_kernel, block_rows=block_rows,...  35.4 us
    pallas_call x1, Pallas kernels, feed_forward(): pl.pallas_call(ff_kernel, grid=(hidden // block,), in_specs=[pl.BlockSpec...  33.2 us
    ppermute x8, waiting for transfers between devices, scatter_half(): other = lax.ppermute(part, axis, [(i, i ^ stride) for i in senders])  23.8 us
  transfers between devices with their start and end apart: 74, of which 30 were waited for; matrix products, arithmetic and copies ran while one was open for 19% of the time, Pallas kernels for 12%

profile of v2, /device:TPU:0, one launch (start us, length us, event | category | flops | bytes accessed | tf_op | source)
XLA Modules:
  0.0 847.4 jit_solution(4335886834971506629)
XLA Ops:
  18.0 13.9 %collective-permute-done.1 = bf16[192,896]{1,0:T(8,128)(2,1)S(1)} collective-permute-done((bf16[192,896]{1,0:T(8,128)(2,1)}, bf16[192,896]{1,0:T(8,128)(2,1)S(1)}, u32[]{:S(2)}, u32[]{:S(2)}) %collective-permute-start.1) | collective-permute-done | bytes 344096 | tf_op jit(solution)/shard_map/ppermute | solution.py:445
  32.0 10.9 %collective-permute-start.2 = (bf16[192,896]{1,0:T(8,128)(2,1)S(1)}, bf16[192,896]{1,0:T(8,128)(2,1)S(1)}, u32[]{:S(2)}, u32[]{:S(2)}) collective-permute-start(bf16[192,896]{1,0:T(8,128)(2,1)S(1)} %get-tuple-element.60), channel_id=1, source_target_pairs={{0,8},{4,12},{8,0},{12,4},{16,24},{20,28},{24,16},{28,20},{1,9},{5... | collective-permute-start | bytes 1032200 | tf_op jit(solution)/shard_map/ppermute | solution.py:445
  42.9 9.8 %collective-permute-done.10 = s32[2,4,128]{2,1,0:T(4,128)S(1)} collective-permute-done((s32[2,4,128]{2,1,0:T(4,128)S(1)}, s32[2,4,128]{2,1,0:T(4,128)S(1)}, u32[]{:S(2)}, u32[]{:S(2)}) %collective-permute-start.10) | collective-permute-done | bytes 4128 | tf_op jit(solution)/shard_map/ppermute | solution.py:445
  68.6 7.4 fusion.7
  78.6 9.5 %collective-permute-done.4 = bf16[2,2,96,896]{3,2,0,1:T(8,128)(2,1)S(1)} collective-permute-done((bf16[2,2,96,896]{3,2,0,1:T(8,128)(2,1)S(1)}, bf16[2,2,96,896]{3,2,0,1:T(8,128)(2,1)S(1)}, u32[]{:S(2)}, u32[]{:S(2)}) %collective-permute-start.4) | collective-permute-done | bytes 688160 | tf_op jit(solution)/shard_map/ppermute | solution.py:445
  100.4 8.8 %proj_self.1 = bf16[8,512,384]{2,1,0:T(8,128)(2,1)} custom-call(bf16[512,896]{1,0:T(8,128)(2,1)} %fusion.12.x_ref, bf16[3072,896]{1,0:T(8,128)(2,1)} %bitcast.17.wq_ref.wk_ref.wv_ref, bf16[3072,896]{1,0:T(8,128)(2,1)} %bitcast.17.wq_ref.wk_ref.wv_ref, bf16[3072,896]{1,0:T(8,128)(2,1)} %bitcast.17.wq_ref.wk_ref.wv_ref, f32[512,128]{1,0:T(8,128)} %bitcast.361, ...), custom_call_target="tpu_custom_call" | custom-call | flops 2818572288 | bytes 9699328 | tf_op jit(solution)/shard_map/proj_self/pallas_call | solution.py:74
  109.2 4.9 all-to-all-start
  116.1 84.3 %collective-permute-done.12 = bf16[192,896]{1,0:T(8,128)(2,1)S(1)} collective-permute-done((bf16[192,896]{1,0:T(8,128)(2,1)S(1)}, bf16[192,896]{1,0:T(8,128)(2,1)S(1)}, u32[]{:S(2)}, u32[]{:S(2)}) %collective-permute-start.12) | collective-permute-done | bytes 344096 | tf_op jit(solution)/shard_map/ppermute | solution.py:445
  204.1 13.3 %collective-permute-done.13 = bf16[2,96,896]{2,1,0:T(8,128)(2,1)S(1)} collective-permute-done((bf16[2,96,896]{2,1,0:T(8,128)(2,1)S(1)}, bf16[2,96,896]{2,1,0:T(8,128)(2,1)S(1)}, u32[]{:S(2)}, u32[]{:S(2)}) %collective-permute-start.13) | collective-permute-done | bytes 344096 | tf_op jit(solution)/shard_map/ppermute | solution.py:445
  220.3 5.8 collective-permute-start.19
  226.7 6.9 collective-permute-done.14
  239.4 6.8 collective-permute-done.17
  261.1 16.8 %attn_self_fwd.1 = bf16[8,4,128,128]{3,2,1,0:T(8,128)(2,1)} custom-call(bf16[8,4,128,384]{3,2,1,0:T(8,128)(2,1)} %bitcast.30.qkv_ref, s32[4,1024,1]{2,1,0:T(8,128)} %copy.93.doc_ref), custom_call_target="tpu_custom_call" | custom-call | flops 4294967296 | bytes 4718592 | tf_op jit(solution)/shard_map/attn_self_fwd/pallas_call | solution.py:219
  280.2 6.5 all-to-all-start.1
  289.3 14.0 %convert_bitcast_fusion.k_ref.v_ref = bf16[2048,2048]{1,0:T(8,128)(2,1)} fusion(bf16[2048,896]{1,0:T(8,128)(2,1)} %bitcast.396, bf16[3072,896]{1,0:T(8,128)(2,1)} %bitcast.50), kind=kOutput, calls=%fused_computation | convolution fusion | flops 7520387072 | bytes 15728640 | tf_op jit(solution)/shard_map/dot_general | solution.py:30
  303.3 9.8 %all-to-all-done.1 = bf16[8,512,128]{1,2,0:T(8,128)(2,1)S(1)} async-done(((bf16[8,512,128]{1,2,0:T(8,128)(2,1)}), bf16[8,512,128]{1,2,0:T(8,128)(2,1)S(1)}, u32[]{:S(2)}, u32[]{:S(2)}) %all-to-all-start.1) | async-done | bytes 1048608 | tf_op jit(solution)/shard_map/all_to_all | solution.py:610
  321.4 44.0 %attn_cross_fwd.1 = bf16[512,1024]{1,0:T(8,128)(2,1)} custom-call(bf16[512,1024]{1,0:T(8,128)(2,1)} %fusion.36.q_ref, bf16[2048,2048]{1,0:T(8,128)(2,1)} %convert_bitcast_fusion.k_ref.v_ref, bf16[2048,2048]{1,0:T(8,128)(2,1)} %convert_bitcast_fusion.k_ref.v_ref, f32[512,1]{1,0:T(8,128)} %copy.100.valid_ref), custom_call_target="tpu_custom_call" | custom-call | flops 1073741824 | bytes 10485760 | tf_op jit(solution)/shard_map/attn_cross_fwd/pallas_call | solution.py:317
  370.8 33.2 %feed_forward.1 = (bf16[512,896]{1,0:T(8,128)(2,1)}, f32[512,896]{1,0:T(8,128)}, bf16[3584,1792]{1,0:T(8,128)(2,1)}) custom-call(bf16[512,896]{1,0:T(8,128)(2,1)} %multiply_convert_fusion.x_ref, bf16[512,896]{1,0:T(8,128)(2,1)} %bitcast.353, bf16[3584,1792]{1,0:T(8,128)(2,1)} %all-gather.5.cloned.1.call-done.win_ref.wdown_ref, ...), custom_call_target="tpu_custom_call" | custom-call | flops 19730006016 | bytes 25690112 | tf_op jit(solution)/shard_map/feed_forward/pallas_call | solution.py:390
  414.4 51.6 %attn_cross_bwd.1 = (bf16[512,1024]{1,0:T(8,128)(2,1)}, bf16[2048,2048]{1,0:T(8,128)(2,1)}) custom-call(bf16[512,1024]{1,0:T(8,128)(2,1)} %fusion.36.q_ref, bf16[2048,2048]{1,0:T(8,128)(2,1)} %convert_bitcast_fusion.k_ref.v_ref, bf16[2048,2048]{1,0:T(8,128)(2,1)} %convert_bitcast_fusion.k_ref.v_ref, f32[512,1]{1,0:T(8,128)} %copy.100.valid_ref, ...), custom_call_target="tpu_custom_call" | custom-call | flops 2684354560 | bytes 19922944 | tf_op jit(solution)/shard_map/attn_cross_bwd/pallas_call | solution.py:333
  492.4 9.6 %convolution_convert_fusion.1 = bf16[2048,896]{1,0:T(8,128)(2,1)S(1)} fusion(bf16[2048,2048]{1,0:T(8,128)(2,1)S(1)} %bitcast.395, bf16[2048,896]{1,0:T(8,128)(2,1)S(1)} %bitcast.397), kind=kOutput, calls=%fused_computation.3 | convolution fusion | flops 7518027776 | bytes 15728640 | tf_op jit(solution)/shard_map/dot_general | solution.py:30
  502.5 14.2 %fusion = f32[2048,896]{1,0:T(8,128)} fusion(bf16[2048,2048]{1,0:T(8,128)(2,1)} %get-tuple-element.16, bf16[3072,896]{1,0:T(8,128)(2,1)} %bitcast.50), kind=kOutput, calls=%fused_computation.4 | convolution fusion | flops 7516192768 | bytes 19398656 | tf_op jit(solution)/shard_map/dot_general | solution.py:30
  532.5 10.4 %collective-permute-done.53 = bf16[2,2,56,512]{3,2,0,1:T(8,128)(2,1)S(1)} collective-permute-done((bf16[2,2,56,512]{3,2,0,1:T(8,128)(2,1)S(1)}, bf16[2,2,56,512]{3,2,0,1:T(8,128)(2,1)S(1)}, u32[]{:S(2)}, u32[]{:S(2)}) %collective-permute-start.53) | collective-permute-done | bytes 229408 | tf_op jit(solution)/shard_map/ppermute | solution.py:445
  545.9 6.2 collective-permute-done.43
  564.7 35.4 %attn_self_bwd.1 = bf16[8,4,128,384]{3,2,1,0:T(8,128)(2,1)} custom-call(bf16[8,4,128,384]{3,2,1,0:T(8,128)(2,1)} %bitcast.30.qkv_ref, bf16[8,4,128,128]{3,2,1,0:T(8,128)(2,1)} %bitcast.58.grad_ref, s32[4,1024,1]{2,1,0:T(8,128)} %copy.93.doc_ref, f32[4,1024,128]{2,1,0:T(8,128)} %copy-done.9, f32[4,1024,128]{2,1,0:T(8,128)} %copy-done.8), custom_call_target="tpu_custom_call" | custom-call | flops 10737418240 | bytes 9437184 | tf_op jit(solution)/shard_map/attn_self_bwd/pallas_call | solution.py:241
  616.2 64.0 %collective-permute-done.60 = bf16[56,512]{1,0:T(8,128)(2,1)S(1)} collective-permute-done((bf16[56,512]{1,0:T(8,128)(2,1)S(1)}, bf16[56,512]{1,0:T(8,128)(2,1)S(1)}, u32[]{:S(2)}, u32[]{:S(2)}) %collective-permute-start.60) | collective-permute-done | bytes 57376 | tf_op jit(solution)/shard_map/ppermute | solution.py:445
  682.9 5.4 collective-permute-start.46
  688.4 9.7 %collective-permute-done.56 = bf16[56,512]{1,0:T(8,128)(2,1)S(1)} collective-permute-done((bf16[56,512]{1,0:T(8,128)(2,1)S(1)}, bf16[56,512]{1,0:T(8,128)(2,1)S(1)}, u32[]{:S(2)}, u32[]{:S(2)}) %collective-permute-start.56) | collective-permute-done | bytes 57376 | tf_op jit(solution)/shard_map/ppermute | solution.py:551
  706.6 9.8 %collective-permute-done.23 = bf16[2,2,96,896]{3,2,0,1:T(8,128)(2,1)S(1)} collective-permute-done((bf16[2,2,96,896]{3,2,0,1:T(8,128)(2,1)S(1)}, bf16[2,2,96,896]{3,2,0,1:T(8,128)(2,1)S(1)}, u32[]{:S(2)}, u32[]{:S(2)}) %collective-permute-start.23) | collective-permute-done | bytes 688160 | tf_op jit(solution)/shard_map/ppermute | solution.py:445
  740.8 6.8 fusion.17
  771.6 17.5 %collective-permute-done.21 = f32[4,63,896]{2,0,1:T(4,128)S(1)} collective-permute-done((f32[4,63,896]{2,0,1:T(4,128)S(1)}, f32[4,63,896]{2,0,1:T(4,128)S(1)}, u32[]{:S(2)}, u32[]{:S(2)}) %collective-permute-start.21) | collective-permute-done | bytes 903200 | tf_op jit(solution)/shard_map/ppermute | solution.py:439
  790.8 13.0 %collective-permute-done.38 = bf16[2,2,96,896]{3,2,0,1:T(8,128)(2,1)S(1)} collective-permute-done((bf16[2,2,96,896]{3,2,0,1:T(8,128)(2,1)S(1)}, bf16[2,2,96,896]{3,2,0,1:T(8,128)(2,1)S(1)}, u32[]{:S(2)}, u32[]{:S(2)}) %collective-permute-start.38) | collective-permute-done | bytes 688160 | tf_op jit(solution)/shard_map/ppermute | solution.py:445
  822.6 11.0 %collective-permute-done.36 = bf16[96,896]{1,0:T(8,128)(2,1)S(1)} collective-permute-done((bf16[96,896]{1,0:T(8,128)(2,1)S(1)}, bf16[96,896]{1,0:T(8,128)(2,1)S(1)}, u32[]{:S(2)}, u32[]{:S(2)}) %collective-permute-start.36) | collective-permute-done | bytes 172064 | tf_op jit(solution)/shard_map/ppermute | solution.py:551
  (394 shorter events, 260.3 us)
Async XLA Ops:
  7.2 296.1 %all-gather.3.cloned.1.call-start = ((), (), s32[]{:S(2)}) async-start(), calls=%async_computation.5 | async-start | bytes 3784704 | tf_op jit(solution)/shard_map/all_gather | solution.py:570
  7.9 362.7 %all-gather.5.cloned.1.call-start = ((), (), s32[]{:S(2)}) async-start(), calls=%async_computation.6 | async-start | bytes 13246464 | tf_op jit(solution)/shard_map/all_gather | solution.py:571
  9.8 22.1 %collective-permute-start.1 = (bf16[192,896]{1,0:T(8,128)(2,1)}, bf16[192,896]{1,0:T(8,128)(2,1)S(1)}, u32[]{:S(2)}, u32[]{:S(2)}) collective-permute-start(bf16[192,896]{1,0:T(8,128)(2,1)} %bitcast.376), channel_id=1, source_target_pairs={{0,16},{4,20},{8,24},{12,28},{16,0},{20,4},{24,8},{28,12},{1,17},{... | collective-permute-start | bytes 1032200 | tf_op jit(solution)/shard_map/ppermute | solution.py:445
  16.5 72.7 %collective-permute-start = (bf16[4,63,896]{2,1,0:T(8,128)(2,1)S(1)}, bf16[4,63,896]{2,1,0:T(8,128)(2,1)}, u32[]{:S(2)}, u32[]{:S(2)}) collective-permute-start(bf16[4,63,896]{2,1,0:T(8,128)(2,1)S(1)} %slice.89), channel_id=1, source_target_pairs={{0,28},{4,0},{8,4},{12,8},{16,12},{20,16},{24,20},{28,24},{1,29},{... | collective-permute-start | bytes 1354760 | tf_op jit(solution)/shard_map/ppermute | solution.py:432
  109.2 151.9 %all-to-all-start = ((bf16[8,512,384]{2,1,0:T(8,128)(2,1)}), bf16[8,512,384]{2,1,0:T(8,128)(2,1)}, u32[]{:S(2)}, u32[]{:S(2)}) async-start(bf16[8,512,384]{2,1,0:T(8,128)(2,1)} %proj_self.1), calls=%async_computation | async-start | bytes 6291456 | tf_op jit(solution)/shard_map/all_to_all | solution.py:607
  114.1 86.3 %collective-permute-start.12 = (bf16[192,896]{1,0:T(8,128)(2,1)S(1)}, bf16[192,896]{1,0:T(8,128)(2,1)S(1)}, u32[]{:S(2)}, u32[]{:S(2)}) collective-permute-start(bf16[192,896]{1,0:T(8,128)(2,1)S(1)} %get-tuple-element.59), channel_id=1, source_target_pairs={{0,8},{4,12},{8,0},{12,4},{16,24},{20,28},{24,16},{28,20},{1,9},{5... | collective-permute-start | bytes 1032200 | tf_op jit(solution)/shard_map/ppermute | solution.py:445
  220.3 29.4 %collective-permute-start.19 = (bf16[4,63,896]{2,1,0:T(8,128)(2,1)}, bf16[4,63,896]{2,1,0:T(8,128)(2,1)}, u32[]{:S(2)}, u32[]{:S(2)}) collective-permute-start(bf16[4,63,896]{2,1,0:T(8,128)(2,1)} %slice.100), channel_id=1, source_target_pairs={{0,28},{4,0},{8,4},{12,8},{16,12},{20,16},{24,20},{28,24},{1,29},{... | collective-permute-start | bytes 1354760 | tf_op jit(solution)/shard_map/ppermute | solution.py:432
  233.8 22.1 %collective-permute-start.15 = (bf16[2,2,2,96,896]{4,3,0,1,2:T(8,128)(2,1)S(1)}, bf16[2,2,2,96,896]{4,3,0,1,2:T(8,128)(2,1)}, u32[]{:S(2)}, u32[]{:S(2)}) collective-permute-start(bf16[2,2,2,96,896]{4,3,0,1,2:T(8,128)(2,1)S(1)} %bitcast_dynamic-update-slice_fusion.1), channel_id=1, source_target_pairs={{0,1},{1,0},{2,3},{3,2},{4,5},{5,4},{6,7},{7,6},{8,9},{9,8},{10,11... | collective-permute-start | bytes 4128776 | tf_op jit(solution)/shard_map/ppermute | solution.py:445
  249.6 37.1 %collective-permute-start.18 = (bf16[2,2,2,96,896]{4,3,0,2,1:T(8,128)(2,1)}, bf16[2,2,2,96,896]{4,3,0,2,1:T(8,128)(2,1)}, u32[]{:S(2)}, u32[]{:S(2)}) collective-permute-start(bf16[2,2,2,96,896]{4,3,0,2,1:T(8,128)(2,1)} %bitcast_dynamic-update-slice_fusion), channel_id=1, source_target_pairs={{0,1},{1,0},{2,3},{3,2},{4,5},{5,4},{6,7},{7,6},{8,9},{9,8},{10,11... | collective-permute-start | bytes 4128776 | tf_op jit(solution)/shard_map/ppermute | solution.py:445
  280.2 32.9 %all-to-all-start.1 = ((bf16[8,512,128]{1,2,0:T(8,128)(2,1)}), bf16[8,512,128]{1,2,0:T(8,128)(2,1)S(1)}, u32[]{:S(2)}, u32[]{:S(2)}) async-start(bf16[8,512,128]{1,2,0:T(8,128)(2,1)} %copy.94), calls=%async_computation.1 | async-start | bytes 2097152 | tf_op jit(solution)/shard_map/all_to_all | solution.py:610
  286.7 551.1 %reduce-scatter.2.cloned.1.call-start = ((), (), s32[]{:S(2)}) async-start(), calls=%async_computation.7 | async-start | bytes 13246464 | tf_op jit(solution)/shard_map/reduce_scatter | solution.py:621
  476.6 88.2 %all-to-all-start.2 = ((bf16[8,512,128]{2,1,0:T(8,128)(2,1)}), bf16[8,512,128]{2,1,0:T(8,128)(2,1)}, u32[]{:S(2)}, u32[]{:S(2)}) async-start(bf16[8,512,128]{2,1,0:T(8,128)(2,1)} %bitcast.352), calls=%async_computation.2 | async-start | bytes 2097152 | tf_op jit(solution)/shard_map/all_to_all | solution.py:640
  484.9 39.7 %collective-permute-start.52 = (bf16[2,2,2,56,512]{4,3,0,1,2:T(8,128)(2,1)S(1)}, bf16[2,2,2,56,512]{4,3,0,1,2:T(8,128)(2,1)}, u32[]{:S(2)}, u32[]{:S(2)}) collective-permute-start(bf16[2,2,2,56,512]{4,3,0,1,2:T(8,128)(2,1)S(1)} %bitcast.373), channel_id=1, source_target_pairs={{0,1},{1,0},{2,3},{3,2},{4,5},{5,4},{6,7},{7,6},{8,9},{9,8},{10,11... | collective-permute-start | bytes 1376264 | tf_op jit(solution)/shard_map/ppermute | solution.py:445
  485.1 41.1 %collective-permute-start.57 = (bf16[2,2,2,56,512]{4,3,0,2,1:T(8,128)(2,1)S(1)}, bf16[2,2,2,56,512]{4,3,0,2,1:T(8,128)(2,1)S(1)}, u32[]{:S(2)}, u32[]{:S(2)}) collective-permute-start(bf16[2,2,2,56,512]{4,3,0,2,1:T(8,128)(2,1)S(1)} %bitcast.372), channel_id=1, source_target_pairs={{0,1},{1,0},{2,3},{3,2},{4,5},{5,4},{6,7},{7,6},{8,9},{9,8},{10,11... | collective-permute-start | bytes 1376264 | tf_op jit(solution)/shard_map/ppermute | solution.py:445
  488.1 40.8 %collective-permute-start.42 = (bf16[2,2,2,56,512]{4,3,0,1,2:T(8,128)(2,1)S(1)}, bf16[2,2,2,56,512]{4,3,0,1,2:T(8,128)(2,1)}, u32[]{:S(2)}, u32[]{:S(2)}) collective-permute-start(bf16[2,2,2,56,512]{4,3,0,1,2:T(8,128)(2,1)S(1)} %bitcast.375), channel_id=1, source_target_pairs={{0,1},{1,0},{2,3},{3,2},{4,5},{5,4},{6,7},{7,6},{8,9},{9,8},{10,11... | collective-permute-start | bytes 1376264 | tf_op jit(solution)/shard_map/ppermute | solution.py:445
  488.4 41.9 %collective-permute-start.47 = (bf16[2,2,2,56,512]{4,3,0,2,1:T(8,128)(2,1)S(1)}, bf16[2,2,2,56,512]{4,3,0,2,1:T(8,128)(2,1)}, u32[]{:S(2)}, u32[]{:S(2)}) collective-permute-start(bf16[2,2,2,56,512]{4,3,0,2,1:T(8,128)(2,1)S(1)} %bitcast.374), channel_id=1, source_target_pairs={{0,1},{1,0},{2,3},{3,2},{4,5},{5,4},{6,7},{7,6},{8,9},{9,8},{10,11... | collective-permute-start | bytes 1376264 | tf_op jit(solution)/shard_map/ppermute | solution.py:445
  489.1 33.4 %collective-permute-start.20 = (bf16[4,63,896]{2,1,0:T(8,128)(2,1)S(1)}, bf16[4,63,896]{2,1,0:T(8,128)(2,1)}, u32[]{:S(2)}, u32[]{:S(2)}) collective-permute-start(bf16[4,63,896]{2,1,0:T(8,128)(2,1)S(1)} %copy-done.19), channel_id=1, source_target_pairs={{0,4},{4,8},{8,12},{12,16},{16,20},{20,24},{24,28},{28,0},{1,5},{5... | collective-permute-start | bytes 1354760 | tf_op jit(solution)/shard_map/ppermute | solution.py:439
  522.5 177.2 %collective-permute-start.22 = (bf16[2,2,2,96,896]{4,3,0,1,2:T(8,128)(2,1)}, bf16[2,2,2,96,896]{4,3,0,1,2:T(8,128)(2,1)}, u32[]{:S(2)}, u32[]{:S(2)}) collective-permute-start(bf16[2,2,2,96,896]{4,3,0,1,2:T(8,128)(2,1)} %bitcast.338), channel_id=1, source_target_pairs={{0,1},{1,0},{2,3},{3,2},{4,5},{5,4},{6,7},{7,6},{8,9},{9,8},{10,11... | collective-permute-start | bytes 4128776 | tf_op jit(solution)/shard_map/ppermute | solution.py:445
  524.6 177.0 %collective-permute-start.27 = (bf16[2,2,2,96,896]{4,3,0,2,1:T(8,128)(2,1)}, bf16[2,2,2,96,896]{4,3,0,2,1:T(8,128)(2,1)}, u32[]{:S(2)}, u32[]{:S(2)}) collective-permute-start(bf16[2,2,2,96,896]{4,3,0,2,1:T(8,128)(2,1)} %bitcast.337), channel_id=1, source_target_pairs={{0,1},{1,0},{2,3},{3,2},{4,5},{5,4},{6,7},{7,6},{8,9},{9,8},{10,11... | collective-permute-start | bytes 4128776 | tf_op jit(solution)/shard_map/ppermute | solution.py:445
  530.2 21.9 %collective-permute-start.43 = (bf16[2,2,56,512]{3,2,0,1:T(8,128)(2,1)S(1)}, bf16[2,2,56,512]{3,2,0,1:T(8,128)(2,1)S(1)}, u32[]{:S(2)}, u32[]{:S(2)}) collective-permute-start(bf16[2,2,56,512]{3,2,0,1:T(8,128)(2,1)S(1)} %dynamic-slice_bitcast_fusion.11), channel_id=1, source_target_pairs={{0,2},{1,3},{2,0},{3,1},{4,6},{5,7},{6,4},{7,5},{8,10},{9,11},{10,... | collective-permute-start | bytes 688136 | tf_op jit(solution)/shard_map/ppermute | solution.py:445
  554.7 54.6 %collective-permute-start.44 = (bf16[2,56,512]{2,1,0:T(8,128)(2,1)S(1)}, bf16[2,56,512]{2,1,0:T(8,128)(2,1)}, u32[]{:S(2)}, u32[]{:S(2)}) collective-permute-start(bf16[2,56,512]{2,1,0:T(8,128)(2,1)S(1)} %dynamic-slice_bitcast_fusion.19), channel_id=1, source_target_pairs={{0,4},{4,0},{8,12},{12,8},{16,20},{20,16},{24,28},{28,24},{1,5},{5... | collective-permute-start | bytes 344072 | tf_op jit(solution)/shard_map/ppermute | solution.py:445
  556.2 56.1 %collective-permute-start.49 = (bf16[2,56,512]{2,1,0:T(8,128)(2,1)}, bf16[2,56,512]{2,1,0:T(8,128)(2,1)}, u32[]{:S(2)}, u32[]{:S(2)}) collective-permute-start(bf16[2,56,512]{2,1,0:T(8,128)(2,1)} %dynamic-slice_bitcast_fusion.18), channel_id=1, source_target_pairs={{0,2},{1,3},{2,0},{3,1},{4,6},{5,7},{6,4},{7,5},{8,10},{9,11},{10,... | collective-permute-start | bytes 344072 | tf_op jit(solution)/shard_map/ppermute | solution.py:445
  561.6 51.9 %collective-permute-start.55 = (bf16[56,512]{1,0:T(8,128)(2,1)}, bf16[56,512]{1,0:T(8,128)(2,1)}, u32[]{:S(2)}, u32[]{:S(2)}) collective-permute-start(bf16[56,512]{1,0:T(8,128)(2,1)} %dynamic-slice_bitcast_fusion.21), channel_id=1, source_target_pairs={{0,8},{4,12},{8,0},{12,4},{16,24},{20,28},{24,16},{28,20},{1,9},{5... | collective-permute-start | bytes 172040 | tf_op jit(solution)/shard_map/ppermute | solution.py:445
  604.9 133.8 %all-to-all-start.3 = ((bf16[8,512,384]{1,2,0:T(8,128)(2,1)}), bf16[8,512,384]{1,2,0:T(8,128)(2,1)}, u32[]{:S(2)}, u32[]{:S(2)}) async-start(bf16[8,512,384]{1,2,0:T(8,128)(2,1)} %copy.104), calls=%async_computation.3 | async-start | bytes 6291456 | tf_op jit(solution)/shard_map/all_to_all | solution.py:649
  609.4 70.9 %collective-permute-start.60 = (bf16[56,512]{1,0:T(8,128)(2,1)S(1)}, bf16[56,512]{1,0:T(8,128)(2,1)S(1)}, u32[]{:S(2)}, u32[]{:S(2)}) collective-permute-start(bf16[56,512]{1,0:T(8,128)(2,1)S(1)} %dynamic-slice_bitcast_fusion.20), channel_id=1, source_target_pairs={{0,8},{4,12},{8,0},{12,4},{16,24},{20,28},{24,16},{28,20},{1,9},{5... | collective-permute-start | bytes 172040 | tf_op jit(solution)/shard_map/ppermute | solution.py:445
  612.3 69.3 %collective-permute-start.45 = (bf16[56,512]{1,0:T(8,128)(2,1)S(1)}, bf16[56,512]{1,0:T(8,128)(2,1)S(1)}, u32[]{:S(2)}, u32[]{:S(2)}) collective-permute-start(bf16[56,512]{1,0:T(8,128)(2,1)S(1)} %dynamic-slice_bitcast_fusion.23), channel_id=1, source_target_pairs={{0,8},{4,12},{8,0},{12,4},{16,24},{20,28},{24,16},{28,20},{1,9},{5... | collective-permute-start | bytes 172040 | tf_op jit(solution)/shard_map/ppermute | solution.py:445
  613.6 69.3 %collective-permute-start.50 = (bf16[56,512]{1,0:T(8,128)(2,1)S(1)}, bf16[56,512]{1,0:T(8,128)(2,1)S(1)}, u32[]{:S(2)}, u32[]{:S(2)}) collective-permute-start(bf16[56,512]{1,0:T(8,128)(2,1)S(1)} %dynamic-slice_bitcast_fusion.22), channel_id=1, source_target_pairs={{0,8},{4,12},{8,0},{12,4},{16,24},{20,28},{24,16},{28,20},{1,9},{5... | collective-permute-start | bytes 172040 | tf_op jit(solution)/shard_map/ppermute | solution.py:445
  733.4 22.8 %collective-permute-start.26 = (bf16[96,896]{1,0:T(8,128)(2,1)S(1)}, bf16[96,896]{1,0:T(8,128)(2,1)S(1)}, u32[]{:S(2)}, u32[]{:S(2)}) collective-permute-start(bf16[96,896]{1,0:T(8,128)(2,1)S(1)} %fusion.74), channel_id=1, source_target_pairs={{0,16},{4,20},{8,24},{12,28},{1,17},{5,21},{9,25},{13,29},{2,18},{... | collective-permute-start | bytes 516104 | tf_op jit(solution)/shard_map/ppermute | solution.py:551
  736.8 34.1 %collective-permute-start.31 = (bf16[96,896]{1,0:T(8,128)(2,1)S(1)}, bf16[96,896]{1,0:T(8,128)(2,1)S(1)}, u32[]{:S(2)}, u32[]{:S(2)}) collective-permute-start(bf16[96,896]{1,0:T(8,128)(2,1)S(1)} %fusion.73), channel_id=1, source_target_pairs={{0,16},{4,20},{8,24},{12,28},{1,17},{5,21},{9,25},{13,29},{2,18},{... | collective-permute-start | bytes 516104 | tf_op jit(solution)/shard_map/ppermute | solution.py:551
  763.8 25.3 %collective-permute-start.21 = (f32[4,63,896]{2,0,1:T(4,128)S(1)}, f32[4,63,896]{2,0,1:T(4,128)S(1)}, u32[]{:S(2)}, u32[]{:S(2)}) collective-permute-start(f32[4,63,896]{2,0,1:T(4,128)S(1)} %copy.117), channel_id=1, source_target_pairs={{0,4},{4,8},{8,12},{12,16},{16,20},{20,24},{24,28},{28,0},{1,5},{5... | collective-permute-start | bytes 2709512 | tf_op jit(solution)/shard_map/ppermute | solution.py:439
  768.5 22.0 %collective-permute-start.33 = (bf16[2,2,96,896]{3,2,0,1:T(8,128)(2,1)S(1)}, bf16[2,2,96,896]{3,2,0,1:T(8,128)(2,1)S(1)}, u32[]{:S(2)}, u32[]{:S(2)}) collective-permute-start(bf16[2,2,96,896]{3,2,0,1:T(8,128)(2,1)S(1)} %dynamic-slice_bitcast_fusion.1), channel_id=1, source_target_pairs={{0,2},{1,3},{2,0},{3,1},{4,6},{5,7},{6,4},{7,5},{8,10},{9,11},{10,... | collective-permute-start | bytes 2064392 | tf_op jit(solution)/shard_map/ppermute | solution.py:445
  769.1 34.8 %collective-permute-start.38 = (bf16[2,2,96,896]{3,2,0,1:T(8,128)(2,1)S(1)}, bf16[2,2,96,896]{3,2,0,1:T(8,128)(2,1)S(1)}, u32[]{:S(2)}, u32[]{:S(2)}) collective-permute-start(bf16[2,2,96,896]{3,2,0,1:T(8,128)(2,1)S(1)} %dynamic-slice_bitcast_fusion), channel_id=1, source_target_pairs={{0,4},{4,0},{8,12},{12,8},{16,20},{20,16},{24,28},{28,24},{1,5},{5... | collective-permute-start | bytes 2064392 | tf_op jit(solution)/shard_map/ppermute | solution.py:445
  (77 other events, 1083.1 us)
Sparse Core Ops, SparseCore 0:
  10.9 78.8 all-gather.2
  93.2 154.1 all-gather.4
  470.5 190.5 reduce-scatter.1
